TPU v7x, 32 devices: a whole 2x2x4 slice. The times are simulated.
32 devices in a mesh: dp: 4 (over z), row: 2 (over x), col: 4 (over y, core).
Axes of the slice: x: 2, y: 2, z: 4, core: 2. Of those that a mesh axis runs over, the one named last changes fastest.
Arguments:
- block_input: bfloat16 [4096, 768], P(('dp', 'col'), 'row'), may hold values from -6 to 6
- span_end: int32 [4096], P('dp'), may hold values from 0 to 1023, as said below
- encoder_attention_gain: float32 [768], P('row'), may hold values from 0.25 to 1.75
- encoder_attention_bias: float32 [768], P('row'), may hold values from -1.75 to 1.75
- encoder_query_key_value: bfloat16 [768, 3, 768], P('row', None, 'col'), may hold values from -0.21875 to 0.21875
- encoder_output_weight: bfloat16 [768, 768], P('col', 'row'), may hold values from -3.5 to 3.5
- encoder_feedforward_gain: float32 [768], P('row'), may hold values from 0.25 to 1.75
- encoder_feedforward_bias: float32 [768], P('row'), may hold values from -1.75 to 1.75
- encoder_up_weight: bfloat16 [768, 3072], P('row', 'col'), may hold values from -0.21875 to 0.21875
- encoder_down_weight: bfloat16 [3072, 768], P('col', 'row'), may hold values from -0.109375 to 0.109375
- projection: bfloat16 [768, 512], P('row', 'col'), may hold values from -0.21875 to 0.21875
- decoder_attention_gain: float32 [512], P('col'), may hold values from 0.25 to 1.75
- decoder_attention_bias: float32 [512], P('col'), may hold values from -1.75 to 1.75
- decoder_query_key_value: bfloat16 [512, 3, 512], P('col', None, 'row'), may hold values from -0.25 to 0.25
- decoder_output_weight: bfloat16 [512, 512], P('row', 'col'), may hold values from -4 to 4
- decoder_feedforward_gain: float32 [512], P('col'), may hold values from 0.25 to 1.75
- decoder_feedforward_bias: float32 [512], P('col'), may hold values from -1.75 to 1.75
- decoder_up_weight: bfloat16 [512, 2048], P('col', 'row'), may hold values from -0.25 to 0.25
- decoder_down_weight: bfloat16 [2048, 512], P('row', 'col'), may hold values from -0.125 to 0.125
- output_cotangent: bfloat16 [4096, 512], P(('dp', 'row'), 'col'), may hold values from -6 to 6
Outputs:
- encoder_output: float32 [4096, 768], P(('dp', 'col'), 'row')
- decoder_output: float32 [4096, 512], P(('dp', 'row'), 'col')
- input_gradient: float32 [4096, 768], P(('dp', 'col'), 'row')
- grad_encoder_attention_gain: float32 [768], P('row')
- grad_encoder_attention_bias: float32 [768], P('row')
- grad_encoder_query_key_value: float32 [768, 3, 768], P('row', None, 'col')
- grad_encoder_output_weight: float32 [768, 768], P('col', 'row')
- grad_encoder_feedforward_gain: float32 [768], P('row')
- grad_encoder_feedforward_bias: float32 [768], P('row')
- grad_encoder_up_weight: float32 [768, 3072], P('row', 'col')
- grad_encoder_down_weight: float32 [3072, 768], P('col', 'row')
- grad_projection: float32 [768, 512], P('row', 'col')
- grad_decoder_attention_gain: float32 [512], P('col')
- grad_decoder_attention_bias: float32 [512], P('col')
- grad_decoder_query_key_value: float32 [512, 3, 512], P('col', None, 'row')
- grad_decoder_output_weight: float32 [512, 512], P('row', 'col')
- grad_decoder_feedforward_gain: float32 [512], P('col')
- grad_decoder_feedforward_bias: float32 [512], P('col')
- grad_decoder_up_weight: float32 [512, 2048], P('col', 'row')
- grad_decoder_down_weight: float32 [2048, 512], P('row', 'col')
Inputs may be any that keep to these rules, and one draw needn't show every extreme that they name: `span_end`: each aligned block of 512 positions of a sequence holds one image piece of 256 consecutive patches that starts at a place between 0 and 256 of the block; a patch's value is its piece's last position, every other token's value is its own position in its sequence.
All inputs are finite; a program needn't handle non-finite values.
Results may differ from a plain program's by a relative error of at most 0.039.
Values may be sent and summed in bfloat16 or wider, within the bound.
No kernel may reach another device: no remote copies, remote signals or barrier semaphores. Data moves between devices by JAX's collectives and lax.ppermute only.
A program may use at most 128 MiB of HBM per device.

v0:
```python
import math

import jax
import jax.numpy as jnp
from jax import lax
from jax.sharding import PartitionSpec as P

D1 = 768
D2 = 512
HD1 = 64
HD2 = 32


EPSILON = 1e-06


def as_sent(array):
    return jax.tree.map(lambda a: a.astype(jnp.bfloat16) if a.dtype == jnp.float32 else a, array)


def collect_col(values):
    return lax.all_gather(values, "col", axis=0, tiled=True)


def collect_row(values):
    return lax.all_gather(values, "row", axis=0, tiled=True)


def gather_tokens(values, feature_axis):
    if feature_axis == "row":
        return collect_col(values)
    return collect_row(values)


def product(left, right, flipped):
    if flipped:
        return lax.dot_general(
            left, right, (((1,), (1,)), ((), ())), preferred_element_type=jnp.float32
        )
    return jnp.dot(left, right, preferred_element_type=jnp.float32)


def weight_grad(inputs, gradients):
    return lax.dot_general(
        inputs, gradients, (((0,), (0,)), ((), ())), preferred_element_type=jnp.float32
    )


def sum_features(gathered, matrix, flipped, feature_axis):

    def partial_term():
        return product(gathered, matrix, flipped)

    if feature_axis == "row":
        return lax.psum_scatter(partial_term(), "row", scatter_dimension=0, tiled=True)
    return lax.psum_scatter(
        partial_term().astype(jnp.bfloat16), "col", scatter_dimension=0, tiled=True
    ).astype(jnp.float32)


def line_sum(totals, feature_axis):
    if feature_axis == "row":
        return lax.psum(totals, "row")
    return lax.psum(totals, "col")


def norm_stats(values, feature_axis, full_width):
    totals = line_sum((jnp.sum(values, 1), jnp.sum(values * values, 1)), feature_axis)
    average = totals[0] / full_width
    variance = totals[1] / full_width - average * average
    inverse = lax.rsqrt(variance + EPSILON)
    return ((values - average[:, None]) * inverse[:, None], inverse)


def norm_backward(incoming, centred, inverse, gain, feature_axis, full_width):
    scaled = incoming * gain
    totals = line_sum((jnp.sum(scaled, 1), jnp.sum(scaled * centred, 1)), feature_axis)
    result = inverse[:, None] * (
        scaled - totals[0][:, None] / full_width - centred * totals[1][:, None] / full_width
    )
    return (result, jnp.sum(incoming * centred, 0), jnp.sum(incoming, 0))


def visit(kv_pair, folder, initial, feature_axis):
    if feature_axis == "row":
        return folder(
            initial,
            jax.tree.map(
                lambda part: lax.all_gather(part, "row", axis=0, tiled=True), as_sent(kv_pair)
            ),
            jnp.int32(0),
        )
    return folder(
        initial,
        jax.tree.map(
            lambda part: lax.all_gather(part, "col", axis=0, tiled=True), as_sent(kv_pair)
        ),
        jnp.int32(0),
    )


def key_sum(kv_pair, feature_axis):
    if feature_axis == "row":
        return jax.tree.map(
            lambda part: part.astype(jnp.float32),
            lax.psum_scatter(as_sent(kv_pair), "row", scatter_dimension=0, tiled=True),
        )
    return jax.tree.map(
        lambda part: part.astype(jnp.float32),
        lax.psum_scatter(as_sent(kv_pair), "col", scatter_dimension=0, tiled=True),
    )


def query_ends(span_ends, row_count, feature_axis):
    position = lax.axis_index("row") if feature_axis == "row" else lax.axis_index("col")
    return lax.dynamic_slice_in_dim(span_ends, position * row_count, row_count, 0)


def split_heads(mixed_rows, head_size):
    row_count = mixed_rows.shape[0]
    columns = mixed_rows.shape[1] // 3
    query_rows = mixed_rows[:, :columns].reshape(row_count, columns // head_size, head_size)
    return (query_rows, (mixed_rows[:, columns : 2 * columns], mixed_rows[:, 2 * columns :]))


def key_blocks(shard_rows, head_count, head_size):
    length = shard_rows[0].shape[0]
    block_rows = math.gcd(length, 512)
    number = length // block_rows
    key_rows = shard_rows[0].reshape(number, block_rows, head_count, head_size)
    value_rows = shard_rows[1].reshape(number, block_rows, head_count, head_size)
    starts = block_rows * lax.iota(jnp.int32, number)
    return (key_rows, value_rows, starts)


def exp_scores(query_rows, key_rows, limits, first_key, scaling):
    scores = (
        jnp.einsum("qhd,khd->hqk", query_rows, key_rows, preferred_element_type=jnp.float32)
        * scaling
    )
    places = first_key + lax.iota(jnp.int32, key_rows.shape[0])
    visible = places[None, None, :] <= limits[None, :, None]
    return jnp.where(visible, jnp.exp(scores), 0.0)


def attend(mixed_rows, span_ends, feature_axis, head_size):
    query_rows, kv_pair = split_heads(mixed_rows, head_size)
    row_count, head_count = (query_rows.shape[0], query_rows.shape[1])
    limits = query_ends(span_ends, row_count, feature_axis)
    scaling = head_size ** (-0.5)

    def folder(carried, shard_rows, offset):
        key_rows, value_rows, starts = key_blocks(shard_rows, head_count, head_size)

        def stepper(running, blockset):
            weights = exp_scores(query_rows, blockset[0], limits, blockset[2], scaling)
            numerator = running[0] + jnp.einsum(
                "hqk,khd->qhd",
                weights.astype(jnp.bfloat16),
                blockset[1],
                preferred_element_type=jnp.float32,
            )
            return ((numerator, running[1] + jnp.sum(weights, 2)), None)

        return lax.scan(stepper, carried, (key_rows, value_rows, starts))[0]

    initial = (
        jnp.zeros((row_count, head_count, head_size), jnp.float32),
        jnp.zeros((head_count, row_count), jnp.float32),
    )
    numerator, denominator = visit(kv_pair, folder, initial, feature_axis)
    attended = (numerator / jnp.transpose(denominator)[:, :, None]).astype(jnp.bfloat16)
    return (numerator, denominator, attended.reshape(row_count, head_count * head_size))


def attend_back(
    attended_grad, mixed_rows, numerator, denominator, span_ends, feature_axis, head_size
):
    query_rows, kv_pair = split_heads(mixed_rows, head_size)
    row_count, head_count = (query_rows.shape[0], query_rows.shape[1])
    columns = head_count * head_size
    limits = query_ends(span_ends, row_count, feature_axis)
    scaling = head_size ** (-0.5)
    incoming = attended_grad.reshape(row_count, head_count, head_size)
    numerator_low = (incoming / jnp.transpose(denominator)[:, :, None]).astype(jnp.bfloat16)
    denominator_grad = -jnp.transpose(jnp.sum(incoming * numerator, 2)) / (
        denominator * denominator
    )
    sequence_rows = span_ends.shape[0]

    def folder(carried, shard_rows, offset):
        key_rows, value_rows, starts = key_blocks(shard_rows, head_count, head_size)
        block_rows = key_rows.shape[1]

        def stepper(running, blockset):
            query_grad, key_all, value_all = running
            weights = exp_scores(query_rows, blockset[0], limits, blockset[2], scaling)
            weights_grad = (
                jnp.einsum(
                    "qhd,khd->hqk", numerator_low, blockset[1], preferred_element_type=jnp.float32
                )
                + denominator_grad[:, :, None]
            )
            scores_low = (weights * weights_grad).astype(jnp.bfloat16)
            query_grad = (
                query_grad
                + jnp.einsum(
                    "hqk,khd->qhd", scores_low, blockset[0], preferred_element_type=jnp.float32
                )
                * scaling
            )
            key_part = (
                jnp.einsum(
                    "hqk,qhd->khd", scores_low, query_rows, preferred_element_type=jnp.float32
                )
                * scaling
            )
            value_part = jnp.einsum(
                "hqk,qhd->khd",
                weights.astype(jnp.bfloat16),
                numerator_low,
                preferred_element_type=jnp.float32,
            )
            key_all = lax.dynamic_update_slice_in_dim(
                key_all,
                lax.dynamic_slice_in_dim(key_all, blockset[2], block_rows, 0) + key_part,
                blockset[2],
                0,
            )
            value_all = lax.dynamic_update_slice_in_dim(
                value_all,
                lax.dynamic_slice_in_dim(value_all, blockset[2], block_rows, 0) + value_part,
                blockset[2],
                0,
            )
            return ((query_grad, key_all, value_all), None)

        return lax.scan(stepper, carried, (key_rows, value_rows, starts))[0]

    initial = (
        jnp.zeros((row_count, head_count, head_size), jnp.float32),
        jnp.zeros((sequence_rows, head_count, head_size), jnp.float32),
        jnp.zeros((sequence_rows, head_count, head_size), jnp.float32),
    )
    query_grad, key_all, value_all = visit(kv_pair, folder, initial, feature_axis)
    key_grad, value_grad = key_sum(
        (key_all.reshape(sequence_rows, columns), value_all.reshape(sequence_rows, columns)),
        feature_axis,
    )
    return jnp.concatenate(
        [query_grad.reshape(row_count, columns), key_grad, value_grad], 1
    ).astype(jnp.bfloat16)


def gelu_exact(values):
    return jax.nn.gelu(values, approximate=False)


def layer_forward(stream, params, span_ends, feature_axis, full_width, head_size):
    other_axis = "col" if feature_axis == "row" else "row"
    first_gain, first_bias, mixing, output, second_gain, second_bias, upward, downward = params
    centred_first, inverse_first = norm_stats(stream, feature_axis, full_width)
    normed_first = (centred_first * first_gain + first_bias).astype(jnp.bfloat16)
    whole_first = gather_tokens(normed_first, feature_axis)
    mixed_rows = sum_features(
        whole_first, mixing.reshape(mixing.shape[0], -1), False, feature_axis
    ).astype(jnp.bfloat16)
    numerator, denominator, attended = attend(mixed_rows, span_ends, feature_axis, head_size)
    whole_attended = gather_tokens(attended, other_axis)
    middle = stream + sum_features(whole_attended, output, False, other_axis)
    centred_second, inverse_second = norm_stats(middle, feature_axis, full_width)
    normed_second = (centred_second * second_gain + second_bias).astype(jnp.bfloat16)
    whole_second = gather_tokens(normed_second, feature_axis)
    hidden = sum_features(whole_second, upward, False, feature_axis)
    active = gelu_exact(hidden).astype(jnp.bfloat16)
    whole_active = gather_tokens(active, other_axis)
    result = middle + sum_features(whole_active, downward, False, other_axis)
    stored = (
        centred_first,
        inverse_first,
        whole_first,
        mixed_rows,
        numerator,
        denominator,
        whole_attended,
        centred_second,
        inverse_second,
        whole_second,
        hidden,
        whole_active,
    )
    return (result, stored)


def layer_backward(out_grad, params, stored, span_ends, feature_axis, full_width, head_size):
    other_axis = "col" if feature_axis == "row" else "row"
    first_gain, first_bias, mixing, output, second_gain, second_bias, upward, downward = params
    (
        centred_first,
        inverse_first,
        whole_first,
        mixed_rows,
        numerator,
        denominator,
        whole_attended,
        centred_second,
        inverse_second,
        whole_second,
        hidden,
        whole_active,
    ) = stored
    whole_down = gather_tokens(out_grad.astype(jnp.bfloat16), feature_axis)
    grad_down = weight_grad(whole_active, whole_down)
    active_grad = sum_features(whole_down, downward, True, feature_axis)
    hidden_low = jax.vjp(gelu_exact, hidden)[1](active_grad)[0].astype(jnp.bfloat16)
    whole_hidden = gather_tokens(hidden_low, other_axis)
    grad_up = weight_grad(whole_second, whole_hidden)
    normed_second_grad = sum_features(whole_hidden, upward, True, other_axis)
    back_second, grad_second_gain, grad_second_bias = norm_backward(
        normed_second_grad, centred_second, inverse_second, second_gain, feature_axis, full_width
    )
    middle_grad = out_grad + back_second
    whole_middle = gather_tokens(middle_grad.astype(jnp.bfloat16), feature_axis)
    grad_output = weight_grad(whole_attended, whole_middle)
    attended_grad = sum_features(whole_middle, output, True, feature_axis)
    mixed_low = attend_back(
        attended_grad, mixed_rows, numerator, denominator, span_ends, feature_axis, head_size
    )
    whole_mixed = gather_tokens(mixed_low, other_axis)
    grad_mixing = weight_grad(whole_first, whole_mixed).reshape(mixing.shape)
    normed_first_grad = sum_features(
        whole_mixed, mixing.reshape(mixing.shape[0], -1), True, other_axis
    )
    back_first, grad_first_gain, grad_first_bias = norm_backward(
        normed_first_grad, centred_first, inverse_first, first_gain, feature_axis, full_width
    )
    return (
        middle_grad + back_first,
        (
            grad_first_gain,
            grad_first_bias,
            grad_mixing,
            grad_output,
            grad_second_gain,
            grad_second_bias,
            grad_up,
            grad_down,
        ),
    )


def per_device(
    block_input,
    span_end,
    encoder_attention_gain,
    encoder_attention_bias,
    encoder_query_key_value,
    encoder_output_weight,
    encoder_feedforward_gain,
    encoder_feedforward_bias,
    encoder_up_weight,
    encoder_down_weight,
    projection,
    decoder_attention_gain,
    decoder_attention_bias,
    decoder_query_key_value,
    decoder_output_weight,
    decoder_feedforward_gain,
    decoder_feedforward_bias,
    decoder_up_weight,
    decoder_down_weight,
    output_cotangent,
):
    encoder_params = (
        encoder_attention_gain,
        encoder_attention_bias,
        encoder_query_key_value,
        encoder_output_weight,
        encoder_feedforward_gain,
        encoder_feedforward_bias,
        encoder_up_weight,
        encoder_down_weight,
    )
    decoder_params = (
        decoder_attention_gain,
        decoder_attention_bias,
        decoder_query_key_value,
        decoder_output_weight,
        decoder_feedforward_gain,
        decoder_feedforward_bias,
        decoder_up_weight,
        decoder_down_weight,
    )
    stream = block_input.astype(jnp.float32)
    encoder_out, encoder_stored = layer_forward(stream, encoder_params, span_end, "row", D1, HD1)
    projected_in = collect_col(encoder_out.astype(jnp.bfloat16))
    decoder_in = sum_features(projected_in, projection, False, "row")
    decoder_out, decoder_stored = layer_forward(
        decoder_in, decoder_params, span_end, "col", D2, HD2
    )
    decoder_stored = layer_forward(
        lax.optimization_barrier(decoder_in), decoder_params, span_end, "col", D2, HD2
    )[1]
    decoder_grad, decoder_grads = layer_backward(
        output_cotangent.astype(jnp.float32),
        decoder_params,
        decoder_stored,
        span_end,
        "col",
        D2,
        HD2,
    )
    decoder_gains = lax.psum(
        (decoder_grads[0], decoder_grads[1], decoder_grads[4], decoder_grads[5]), ("dp", "row")
    )
    whole_projected = collect_row(decoder_grad.astype(jnp.bfloat16))
    projection_grad = weight_grad(projected_in, whole_projected)
    encoder_grad = sum_features(whole_projected, projection, True, "col")
    encoder_stored = layer_forward(
        lax.optimization_barrier(stream), encoder_params, span_end, "row", D1, HD1
    )[1]
    input_grad, encoder_grads = layer_backward(
        encoder_grad, encoder_params, encoder_stored, span_end, "row", D1, HD1
    )
    encoder_gains = lax.psum(
        (encoder_grads[0], encoder_grads[1], encoder_grads[4], encoder_grads[5]), ("dp", "col")
    )
    summed = (
        lax.psum(encoder_grads[2].astype(jnp.bfloat16), "dp").astype(jnp.float32),
        lax.psum(encoder_grads[3].astype(jnp.bfloat16), "dp").astype(jnp.float32),
        lax.psum(encoder_grads[6].astype(jnp.bfloat16), "dp").astype(jnp.float32),
        lax.psum(encoder_grads[7].astype(jnp.bfloat16), "dp").astype(jnp.float32),
        lax.psum(projection_grad.astype(jnp.bfloat16), "dp").astype(jnp.float32),
        lax.psum(decoder_grads[2].astype(jnp.bfloat16), "dp").astype(jnp.float32),
        lax.psum(decoder_grads[3].astype(jnp.bfloat16), "dp").astype(jnp.float32),
        lax.psum(decoder_grads[6].astype(jnp.bfloat16), "dp").astype(jnp.float32),
        lax.psum(decoder_grads[7].astype(jnp.bfloat16), "dp").astype(jnp.float32),
    )
    encoder_weights = summed[:5]
    decoder_weights = summed[5:]
    return (
        encoder_out,
        decoder_out,
        input_grad,
        encoder_gains[0],
        encoder_gains[1],
        encoder_weights[0],
        encoder_weights[1],
        encoder_gains[2],
        encoder_gains[3],
        encoder_weights[2],
        encoder_weights[3],
        encoder_weights[4],
        decoder_gains[0],
        decoder_gains[1],
        decoder_weights[0],
        decoder_weights[1],
        decoder_gains[2],
        decoder_gains[3],
        decoder_weights[2],
        decoder_weights[3],
    )


def solution(mesh):
    in_specs = (
        P(("dp", "col"), "row"),
        P("dp"),
        P("row"),
        P("row"),
        P("row", None, "col"),
        P("col", "row"),
        P("row"),
        P("row"),
        P("row", "col"),
        P("col", "row"),
        P("row", "col"),
        P("col"),
        P("col"),
        P("col", None, "row"),
        P("row", "col"),
        P("col"),
        P("col"),
        P("col", "row"),
        P("row", "col"),
        P(("dp", "row"), "col"),
    )
    out_specs = (
        P(("dp", "col"), "row"),
        P(("dp", "row"), "col"),
        P(("dp", "col"), "row"),
        P("row"),
        P("row"),
        P("row", None, "col"),
        P("col", "row"),
        P("row"),
        P("row"),
        P("row", "col"),
        P("col", "row"),
        P("row", "col"),
        P("col"),
        P("col"),
        P("col", None, "row"),
        P("row", "col"),
        P("col"),
        P("col"),
        P("col", "row"),
        P("row", "col"),
    )
    return jax.shard_map(
        per_device, mesh=mesh, in_specs=in_specs, out_specs=out_specs, check_vma=False
    )
```

profile of v0, /device:TPU:0, one launch (start us, length us, event | category | flops | bytes accessed | tf_op | source)
XLA Modules:
  0.0 1365.1 jit_solution(14826692255661460471)
XLA Ops:
  16.6 9.2 all_gather.106
  28.1 8.7 all_gather.129
  41.2 22.1 %reduce-scatter.29.cloned.1.call-done = f32[512,576]{0,1:T(8,128)} async-done(((f32[1024,576]{0,1:T(8,128)}), f32[512,576]{0,1:T(8,128)}) %reduce-scatter.29.cloned.1.call-update) | async-done | bytes 1179664 | tf_op jit(solution)/shard_map/reduce_scatter | solution.py:55
  64.6 7.3 all_gather.108
  72.3 11.9 all_gather.107
  84.5 7.9 while.82
  92.5 11.6 all_gather.109
  110.1 7.3 all_gather.131
  117.8 6.5 all_gather.130
  124.6 7.9 while.86
  132.6 6.5 all_gather.132
  142.4 22.2 %reduce-scatter.69.cloned.1.call-done = bf16[256,384]{1,0:T(8,128)(2,1)} async-done(((bf16[1024,384]{1,0:T(8,128)(2,1)}), bf16[256,384]{1,0:T(8,128)(2,1)}) %reduce-scatter.69.cloned.1.call-update) | async-done | bytes 196624 | tf_op jit(solution)/shard_map/reduce_scatter | solution.py:56
  172.5 7.4 all_gather.110
  182.9 44.4 %reduce-scatter.33.cloned.1.call-done = f32[512,768]{1,0:T(8,128)} async-done(((f32[1024,768]{1,0:T(8,128)}), f32[512,768]{1,0:T(8,128)}) %reduce-scatter.33.cloned.1.call-update) | async-done | bytes 1572880 | tf_op jit(solution)/shard_map/reduce_scatter | solution.py:55
  232.7 27.3 %all-gather.9.cloned.1.call-done = bf16[1024,768]{1,0:T(8,128)(2,1)} async-done(((bf16[512,768]{1,0:T(8,128)(2,1)}), bf16[1024,768]{1,0:T(8,128)(2,1)}) %all-gather.9.cloned.1.call-update) | async-done | bytes 1572880 | tf_op jit(solution)/shard_map/all_gather | solution.py:26
  263.3 23.4 %reduce-scatter.35.cloned.1.call-done = bf16[256,384]{1,0:T(8,128)(2,1)} async-done(((bf16[1024,384]{1,0:T(8,128)(2,1)}), bf16[256,384]{1,0:T(8,128)(2,1)}) %reduce-scatter.35.cloned.1.call-update) | async-done | bytes 196624 | tf_op jit(solution)/shard_map/reduce_scatter | solution.py:56
  288.4 8.3 all_gather.112
  299.1 14.8 %reduce-scatter.37.cloned.1.call-done = f32[512,128]{1,0:T(8,128)} async-done(((f32[1024,128]{1,0:T(8,128)}), f32[512,128]{1,0:T(8,128)}) %reduce-scatter.37.cloned.1.call-update) | async-done | bytes 262160 | tf_op jit(solution)/shard_map/reduce_scatter | solution.py:55
  315.1 6.9 all-reduce.5
  332.0 26.8 %reduce-scatter.47.cloned.1.call-done = bf16[256,768]{1,0:T(8,128)(2,1)} async-done(((bf16[1024,768]{1,0:T(8,128)(2,1)}), bf16[256,768]{1,0:T(8,128)(2,1)}) %reduce-scatter.47.cloned.1.call-update) | async-done | bytes 393232 | tf_op jit(solution)/shard_map/reduce_scatter | solution.py:56
  359.9 6.8 all_gather.121
  367.4 7.3 all_gather.120
  376.1 11.3 while.84
  387.5 7.4 all_gather.122
  396.9 15.0 %reduce-scatter.49.cloned.1.call-done = f32[512,128]{1,0:T(8,128)} async-done(((f32[1024,128]{1,0:T(8,128)}), f32[512,128]{1,0:T(8,128)}) %reduce-scatter.49.cloned.1.call-update) | async-done | bytes 262160 | tf_op jit(solution)/shard_map/reduce_scatter | solution.py:55
  413.1 6.9 all-reduce.4
  438.4 21.0 %reduce-scatter.51.cloned.1.call-done = bf16[256,1024]{1,0:T(8,128)(2,1)} async-done(((bf16[1024,1024]{1,0:T(8,128)(2,1)}), bf16[256,1024]{1,0:T(8,128)(2,1)}) %reduce-scatter.51.cloned.1.call-update) | async-done | bytes 524304 | tf_op jit(solution)/shard_map/reduce_scatter | solution.py:56
  463.9 29.3 %reduce-scatter.53.cloned.1.call-done = bf16[256,1024]{1,0:T(8,128)(2,1)} async-done(((bf16[1024,1024]{1,0:T(8,128)(2,1)}), bf16[256,1024]{1,0:T(8,128)(2,1)}) %reduce-scatter.53.cloned.1.call-update) | async-done | bytes 524304 | tf_op jit(solution)/shard_map/reduce_scatter | solution.py:56
  496.0 22.7 %all-gather.13.cloned.1.call-done = bf16[1024,1024]{1,0:T(8,128)(2,1)} async-done(((bf16[256,1024]{1,0:T(8,128)(2,1)}), bf16[1024,1024]{1,0:T(8,128)(2,1)}) %all-gather.13.cloned.1.call-update) | async-done | bytes 2097168 | tf_op jit(solution)/shard_map/all_gather | solution.py:22
  522.1 14.4 %reduce-scatter.55.cloned.1.call-done = f32[512,128]{1,0:T(8,128)} async-done(((f32[1024,128]{1,0:T(8,128)}), f32[512,128]{1,0:T(8,128)}) %reduce-scatter.55.cloned.1.call-update) | async-done | bytes 262160 | tf_op jit(solution)/shard_map/reduce_scatter | solution.py:55
  538.4 7.5 all-reduce.3
  555.5 20.9 %reduce-scatter.57.cloned.1.call-done = bf16[256,256]{1,0:T(8,128)(2,1)} async-done(((bf16[1024,256]{1,0:T(8,128)(2,1)}), bf16[256,256]{1,0:T(8,128)(2,1)}) %reduce-scatter.57.cloned.1.call-update) | async-done | bytes 131088 | tf_op jit(solution)/shard_map/reduce_scatter | solution.py:56
  580.0 34.5 %while.85 = (s32[]{:T(128)}, f32[256,8,32]{0,2,1:T(8,128)}, f32[1024,8,32]{0,2,1:T(8,128)S(1)}, f32[1024,8,32]{0,2,1:T(8,128)}, bf16[2,512,8,32]{1,3,2,0:T(8,128...) while((s32[]{:T(128)}, f32[256,8,32]{0,2,1:T(8,128)}, ...), condition=%wide.region_54.55_spmd.clone, body=%wide.region_53.54_spmd.clone.sunk | while | flops 344654336 | bytes 29504768 | solution.py:238
  618.5 19.8 %reduce-scatter.61.cloned.1.call-done = bf16[256,256]{0,1:T(8,128)(2,1)} async-done(((bf16[1024,256]{0,1:T(8,128)(2,1)}), bf16[256,256]{0,1:T(8,128)(2,1)}) %reduce-scatter.61.cloned.1.call-update) | async-done | bytes 131088 | tf_op jit(solution)/shard_map/reduce_scatter | solution.py:110
  638.4 24.6 %reduce-scatter.59.cloned.1.call-done = bf16[256,256]{0,1:T(8,128)(2,1)} async-done(((bf16[1024,256]{0,1:T(8,128)(2,1)}), bf16[256,256]{0,1:T(8,128)(2,1)}) %reduce-scatter.59.cloned.1.call-update) | async-done | bytes 131088 | tf_op jit(solution)/shard_map/reduce_scatter | solution.py:110
  664.8 20.1 %all-gather.15.cloned.1.call-done = bf16[1024,768]{0,1:T(8,128)(2,1)} async-done(((bf16[256,768]{0,1:T(8,128)(2,1)}), bf16[1024,768]{0,1:T(8,128)(2,1)}) %all-gather.15.cloned.1.call-update) | async-done | bytes 1572880 | tf_op jit(solution)/shard_map/all_gather | solution.py:22
  687.8 14.6 %reduce-scatter.63.cloned.1.call-done = f32[512,128]{1,0:T(8,128)} async-done(((f32[1024,128]{1,0:T(8,128)}), f32[512,128]{1,0:T(8,128)}) %reduce-scatter.63.cloned.1.call-update) | async-done | bytes 262160 | tf_op jit(solution)/shard_map/reduce_scatter | solution.py:55
  712.2 28.3 %reduce-scatter.39.cloned.1.call-done = bf16[256,768]{1,0:T(8,128)(2,1)} async-done(((bf16[1024,768]{1,0:T(8,128)(2,1)}), bf16[256,768]{1,0:T(8,128)(2,1)}) %reduce-scatter.39.cloned.1.call-update) | async-done | bytes 393232 | tf_op jit(solution)/shard_map/reduce_scatter | solution.py:56
  742.2 6.9 all_gather.115
  750.6 7.3 all_gather.114
  758.6 11.3 while.83
  770.0 7.4 all_gather.116
  778.7 15.0 %reduce-scatter.41.cloned.1.call-done = f32[512,128]{1,0:T(8,128)} async-done(((f32[1024,128]{1,0:T(8,128)}), f32[512,128]{1,0:T(8,128)}) %reduce-scatter.41.cloned.1.call-update) | async-done | bytes 262160 | tf_op jit(solution)/shard_map/reduce_scatter | solution.py:55
  794.9 7.6 all-reduce.2
  810.6 7.7 all_gather.133
  822.0 11.0 reduce-scatter.65.cloned.1.call-done
  833.0 8.4 all_gather.134
  845.1 33.7 %reduce-scatter.71.cloned.1.call-done = f32[512,768]{1,0:T(8,128)} async-done(((f32[1024,768]{1,0:T(8,128)}), f32[512,768]{1,0:T(8,128)}) %reduce-scatter.71.cloned.1.call-update) | async-done | bytes 1572880 | tf_op jit(solution)/shard_map/reduce_scatter | solution.py:55
  884.4 39.9 %reduce-scatter.73.cloned.1.call-done = f32[512,768]{1,0:T(8,128)} async-done(((f32[1024,768]{1,0:T(8,128)}), f32[512,768]{1,0:T(8,128)}) %reduce-scatter.73.cloned.1.call-update) | async-done | bytes 1572880 | tf_op jit(solution)/shard_map/reduce_scatter | solution.py:55
  927.8 27.3 %all-gather.17.cloned.1.call-done = bf16[1024,768]{1,0:T(8,128)(2,1)} async-done(((bf16[512,768]{1,0:T(8,128)(2,1)}), bf16[1024,768]{1,0:T(8,128)(2,1)}) %all-gather.17.cloned.1.call-update) | async-done | bytes 1572880 | tf_op jit(solution)/shard_map/all_gather | solution.py:26
  958.4 23.3 %reduce-scatter.75.cloned.1.call-done = bf16[256,384]{1,0:T(8,128)(2,1)} async-done(((bf16[1024,384]{1,0:T(8,128)(2,1)}), bf16[256,384]{1,0:T(8,128)(2,1)}) %reduce-scatter.75.cloned.1.call-update) | async-done | bytes 196624 | tf_op jit(solution)/shard_map/reduce_scatter | solution.py:56
  990.4 7.6 all_gather.136
  1009.3 9.7 reduce-scatter.77.cloned.1.call-done
  1021.8 28.2 %while.87 = (s32[]{:T(128)}, f32[512,3,64]{0,2,1:T(8,128)S(1)}, f32[1024,3,64]{0,2,1:T(8,128)S(1)}, f32[1024,3,64]{0,2,1:T(8,128)}, bf16[2,512,3,64]{1,3,2,0:T(8...) while((s32[]{:T(128)}, f32[512,3,64]{0,2,1:T(8,128)S(1)}, ...), condition=%wide.region_86.87_spmd.clone, body=%wide.region_85.86_spmd.clone.sunk | while | flops 510460416 | bytes 23410944 | solution.py:238
  1058.2 11.0 reduce-scatter.81.cloned.1.call-done
  1069.2 15.9 %reduce-scatter.79.cloned.1.call-done = bf16[512,192]{0,1:T(8,128)(2,1)} async-done(((bf16[1024,192]{0,1:T(8,128)(2,1)}), bf16[512,192]{0,1:T(8,128)(2,1)}) %reduce-scatter.79.cloned.1.call-update) | async-done | bytes 196624 | tf_op jit(solution)/shard_map/reduce_scatter | solution.py:106
  1087.8 22.1 %all-gather.11.cloned.1.call-done = bf16[1024,1024]{1,0:T(8,128)(2,1)} async-done(((bf16[256,1024]{1,0:T(8,128)(2,1)}), bf16[1024,1024]{1,0:T(8,128)(2,1)}) %all-gather.11.cloned.1.call-update) | async-done | bytes 2097168 | tf_op jit(solution)/shard_map/all_gather | solution.py:22
  1114.2 20.4 %all-gather.23.cloned.1.call-done = bf16[1024,1024]{1,0:T(8,128)(2,1)} async-done(((bf16[256,1024]{1,0:T(8,128)(2,1)}), bf16[1024,1024]{1,0:T(8,128)(2,1)}) %all-gather.23.cloned.1.call-update) | async-done | bytes 2097168 | tf_op jit(solution)/shard_map/all_gather | solution.py:22
  1138.6 20.8 %all-gather.19.cloned.1.call-done = bf16[1024,576]{0,1:T(8,128)(2,1)} async-done(((bf16[512,576]{0,1:T(8,128)(2,1)}), bf16[1024,576]{0,1:T(8,128)(2,1)}) %all-gather.19.cloned.1.call-update) | async-done | bytes 1179664 | tf_op jit(solution)/shard_map/all_gather | solution.py:26
  1167.0 21.8 %all-gather.21.cloned.1.call-done = bf16[1024,768]{1,0:T(8,128)(2,1)} async-done(((bf16[512,768]{1,0:T(8,128)(2,1)}), bf16[1024,768]{1,0:T(8,128)(2,1)}) %all-gather.21.cloned.1.call-update) | async-done | bytes 1572880 | tf_op jit(solution)/shard_map/all_gather | solution.py:26
  1197.1 21.1 %all-reduce.1 = (f32[128]{0:T(128)}, f32[128]{0:T(128)}, f32[128]{0:T(128)}, f32[128]{0:T(128)}) all-reduce(f32[128]{0:T(128)S(1)} %copy-done.121, f32[128]{0:T(128)S(1)} %copy-done.122, f32[128]{0:T(128)S(1)} %copy-done.113, f32[128]{0:T(128)S(1)} %copy-done.114), channel_id=1, replica_groups=mesh['dp'=4,'row'=2,'col'=4] {'dp','row'}, use_global_device_ids=true, to_apply=%region_108.109 | all-reduce | flops 512 | bytes 4096 | tf_op jit(solution)/shard_map/psum | solution.py:413
  1219.9 13.0 reduce-scatter.83.cloned.1.call-done
  1234.1 35.1 %all-reduce = (f32[384]{0:T(512)}, f32[384]{0:T(512)}, f32[384]{0:T(512)}, f32[384]{0:T(512)}) all-reduce(f32[384]{0:T(512)S(1)} %get-tuple-element.634, f32[384]{0:T(512)S(1)} %get-tuple-element.661, f32[384]{0:T(512)S(1)} %copy-done.104, f32[384]{0:T(512)S(1)} %copy-done.105), channel_id=1, replica_groups=mesh['dp'=4,'row'=2,'col'=4] {'dp','col'}, use_global_device_ids=true, to_apply=%region_95.96 | all-reduce | flops 1536 | bytes 12288 | tf_op jit(solution)/shard_map/psum | solution.py:425
  1276.0 70.3 %all-reduce.13.cloned.1.call-done = (bf16[128,3,256]{0,2,1:T(8,128)(2,1)}, bf16[384,3,192]{0,2,1:T(8,128)(2,1)}, bf16[192,384]{1,0:T(8,128)(2,1)}, bf16[384,768]...) async-done(((bf16[128,3,256]{0,2,1:T(8,128)(2,1)}, ...) | async-done | bytes 2654224 | tf_op jit(solution)/shard_map/psum | solution.py:434
  (577 shorter events, 336.9 us)
Async XLA Ops:
  7.2 172.8 %copy-start = (bf16[384,768]{1,0:T(8,128)(2,1)S(1)}, bf16[384,768]{1,0:T(8,128)(2,1)}, u32[]{:S(2)}) copy-start(bf16[384,768]{1,0:T(8,128)(2,1)} %param.40) | copy-start | bytes 1769476
  7.2 56.0 %reduce-scatter.29.cloned.1.call-start = ((), (), s32[]{:S(2)}) async-start(), calls=%async_computation.28 | async-start | bytes 3538944 | tf_op jit(solution)/shard_map/reduce_scatter | solution.py:55
  9.4 155.2 %copy-start.1 = (f32[256,384]{1,0:T(8,128)}, f32[256,384]{1,0:T(8,128)S(1)}, u32[]{:S(2)}) copy-start(f32[256,384]{1,0:T(8,128)S(1)} %convert_element_type.268) | copy-start | bytes 1179652
  28.0 80.7 %reduce-scatter.67.cloned.1.call-start = ((), (), s32[]{:S(2)}) async-start(), calls=%async_computation.51 | async-start | bytes 3538944 | tf_op jit(solution)/shard_map/reduce_scatter | solution.py:55
  39.9 101.4 %reduce-scatter.31.cloned.1.call-start = ((), (), s32[]{:S(2)}) async-start(), calls=%async_computation.29 | async-start | bytes 983040 | tf_op jit(solution)/shard_map/reduce_scatter | solution.py:56
  105.5 59.1 %reduce-scatter.69.cloned.1.call-start = ((), (), s32[]{:S(2)}) async-start(), calls=%async_computation.52 | async-start | bytes 983040 | tf_op jit(solution)/shard_map/reduce_scatter | solution.py:56
  141.2 86.1 %reduce-scatter.33.cloned.1.call-start = ((), (), s32[]{:S(2)}) async-start(), calls=%async_computation.30 | async-start | bytes 4718592 | tf_op jit(solution)/shard_map/reduce_scatter | solution.py:55
  182.6 77.4 %copy-start.59 = (bf16[768,384]{1,0:T(8,128)(2,1)S(1)}, bf16[768,384]{1,0:T(8,128)(2,1)}, u32[]{:S(2)}) copy-start(bf16[768,384]{1,0:T(8,128)(2,1)} %param.41) | copy-start | bytes 1769476
  182.6 77.3 %all-gather.9.cloned.1.call-start = ((), (), s32[]{:S(2)}) async-start(), calls=%async_computation.31 | async-start | bytes 2359296 | tf_op jit(solution)/shard_map/all_gather | solution.py:26
  232.6 54.1 %copy-start.47 = (bf16[256,384]{1,0:T(8,128)(2,1)S(1)}, bf16[256,384]{1,0:T(8,128)(2,1)}, u32[]{:S(2)}) copy-start(bf16[256,384]{1,0:T(8,128)(2,1)} %reduce-scatter.31.cloned.1.call-done) | copy-start | bytes 589828
  232.6 54.1 %reduce-scatter.35.cloned.1.call-start = ((), (), s32[]{:S(2)}) async-start(), calls=%async_computation.32 | async-start | bytes 983040 | tf_op jit(solution)/shard_map/reduce_scatter | solution.py:56
  263.3 50.6 %reduce-scatter.37.cloned.1.call-start = ((), (), s32[]{:S(2)}) async-start(), calls=%async_computation.33 | async-start | bytes 786432 | tf_op jit(solution)/shard_map/reduce_scatter | solution.py:55
  298.8 59.9 %reduce-scatter.47.cloned.1.call-start = ((), (), s32[]{:S(2)}) async-start(), calls=%async_computation.39 | async-start | bytes 1966080 | tf_op jit(solution)/shard_map/reduce_scatter | solution.py:56
  331.3 80.6 %reduce-scatter.49.cloned.1.call-start = ((), (), s32[]{:S(2)}) async-start(), calls=%async_computation.40 | async-start | bytes 786432 | tf_op jit(solution)/shard_map/reduce_scatter | solution.py:55
  396.9 62.5 %reduce-scatter.51.cloned.1.call-start = ((), (), s32[]{:S(2)}) async-start(), calls=%async_computation.41 | async-start | bytes 2621440 | tf_op jit(solution)/shard_map/reduce_scatter | solution.py:56
  428.7 64.6 %reduce-scatter.53.cloned.1.call-start = ((), (), s32[]{:S(2)}) async-start(), calls=%async_computation.42 | async-start | bytes 2621440 | tf_op jit(solution)/shard_map/reduce_scatter | solution.py:56
  437.9 80.8 %all-gather.13.cloned.1.call-start = ((), (), s32[]{:S(2)}) async-start(), calls=%async_computation.43 | async-start | bytes 2621440 | tf_op jit(solution)/shard_map/all_gather | solution.py:22
  495.9 40.6 %copy-start.87 = (f32[512]{0:T(512)S(1)}, f32[512]{0:T(512)}, u32[]{:S(2)}) copy-start(f32[512]{0:T(512)} %copy-done.86) | copy-start | bytes 6148
  496.0 40.6 %copy-start.89 = (f32[512]{0:T(512)S(1)}, f32[512]{0:T(512)}, u32[]{:S(2)}) copy-start(f32[512]{0:T(512)} %copy-done.88) | copy-start | bytes 6148
  496.0 40.6 %copy-start.102 = (f32[128]{0:T(128)S(1)}, f32[128]{0:T(128)}, u32[]{:S(2)}) copy-start(f32[128]{0:T(128)} %param.47) | copy-start | bytes 1540
  496.0 49.9 %copy-start.73 = (bf16[512,128]{1,0:T(8,128)(2,1)S(1)}, bf16[512,128]{1,0:T(8,128)(2,1)}, u32[]{:S(2)}) copy-start(bf16[512,128]{1,0:T(8,128)(2,1)} %param.51) | copy-start | bytes 393220
  496.0 40.5 %reduce-scatter.55.cloned.1.call-start = ((), (), s32[]{:S(2)}) async-start(), calls=%async_computation.44 | async-start | bytes 786432 | tf_op jit(solution)/shard_map/reduce_scatter | solution.py:55
  521.8 54.6 %reduce-scatter.57.cloned.1.call-start = ((), (), s32[]{:S(2)}) async-start(), calls=%async_computation.45 | async-start | bytes 655360 | tf_op jit(solution)/shard_map/reduce_scatter | solution.py:56
  555.5 82.9 %reduce-scatter.61.cloned.1.call-start = ((), (), s32[]{:S(2)}) async-start(), calls=%async_computation.47 | async-start | bytes 655360 | tf_op jit(solution)/shard_map/reduce_scatter | solution.py:110
  616.5 46.4 %reduce-scatter.59.cloned.1.call-start = ((), (), s32[]{:S(2)}) async-start(), calls=%async_computation.46 | async-start | bytes 655360 | tf_op jit(solution)/shard_map/reduce_scatter | solution.py:110
  616.6 68.3 %copy-start.31 = (bf16[128,3,256]{0,2,1:T(8,128)(2,1)S(1)}, bf16[128,3,256]{0,2,1:T(8,128)(2,1)}, u32[]{:S(2)}) copy-start(bf16[128,3,256]{0,2,1:T(8,128)(2,1)} %copy-done.30) | copy-start | bytes 589828
  617.5 67.4 %all-gather.15.cloned.1.call-start = ((), (), s32[]{:S(2)}) async-start(), calls=%async_computation.48 | async-start | bytes 1966080 | tf_op jit(solution)/shard_map/all_gather | solution.py:22
  664.7 37.7 %copy-start.6 = (f32[512,128]{1,0:T(8,128)S(1)}, f32[512,128]{1,0:T(8,128)}, u32[]{:S(2)}) copy-start(f32[512,128]{1,0:T(8,128)} %reduce-scatter.37.cloned.1.call-done) | copy-start | bytes 786436
  664.7 37.7 %copy-start.81 = (f32[512]{0:T(512)S(1)}, f32[512]{0:T(512)}, u32[]{:S(2)}) copy-start(f32[512]{0:T(512)} %copy-done.80) | copy-start | bytes 6148
  664.7 37.7 %copy-start.84 = (f32[512]{0:T(512)S(1)}, f32[512]{0:T(512)}, u32[]{:S(2)}) copy-start(f32[512]{0:T(512)} %copy-done.83) | copy-start | bytes 6148
  664.7 37.7 %copy-start.107 = (f32[128]{0:T(128)S(1)}, f32[128]{0:T(128)}, u32[]{:S(2)}) copy-start(f32[128]{0:T(128)} %param.43) | copy-start | bytes 1540
  664.7 37.7 %copy-start.120 = (f32[128]{0:T(128)S(1)}, f32[128]{0:T(128)}, u32[]{:S(2)}) copy-start(f32[128]{0:T(128)} %param.44) | copy-start | bytes 1540
  664.8 37.7 %reduce-scatter.63.cloned.1.call-start = ((), (), s32[]{:S(2)}) async-start(), calls=%async_computation.49 | async-start | bytes 786432 | tf_op jit(solution)/shard_map/reduce_scatter | solution.py:55
  687.7 52.7 %reduce-scatter.39.cloned.1.call-start = ((), (), s32[]{:S(2)}) async-start(), calls=%async_computation.34 | async-start | bytes 1966080 | tf_op jit(solution)/shard_map/reduce_scatter | solution.py:56
  712.1 81.7 %reduce-scatter.41.cloned.1.call-start = ((), (), s32[]{:S(2)}) async-start(), calls=%async_computation.35 | async-start | bytes 786432 | tf_op jit(solution)/shard_map/reduce_scatter | solution.py:55
  778.6 54.4 %reduce-scatter.65.cloned.1.call-start = ((), (), s32[]{:S(2)}) async-start(), calls=%async_computation.50 | async-start | bytes 983040 | tf_op jit(solution)/shard_map/reduce_scatter | solution.py:56
  794.9 205.6 %copy-start.36 = (f32[512,128]{1,0:T(8,128)}, f32[512,128]{1,0:T(8,128)S(1)}, u32[]{:S(2)}) copy-start(f32[512,128]{1,0:T(8,128)S(1)} %get-tuple-element.821) | copy-start | bytes 786436
  810.5 68.2 %reduce-scatter.71.cloned.1.call-start = ((), (), s32[]{:S(2)}) async-start(), calls=%async_computation.53 | async-start | bytes 4718592 | tf_op jit(solution)/shard_map/reduce_scatter | solution.py:55
  821.9 102.3 %reduce-scatter.73.cloned.1.call-start = ((), (), s32[]{:S(2)}) async-start(), calls=%async_computation.54 | async-start | bytes 4718592 | tf_op jit(solution)/shard_map/reduce_scatter | solution.py:55
  845.0 110.0 %all-gather.17.cloned.1.call-start = ((), (), s32[]{:S(2)}) async-start(), calls=%async_computation.55 | async-start | bytes 2359296 | tf_op jit(solution)/shard_map/all_gather | solution.py:26
  878.8 45.5 %copy-start.16 = (f32[512,768]{1,0:T(8,128)S(1)}, f32[512,768]{1,0:T(8,128)}, u32[]{:S(2)}) copy-start(f32[512,768]{1,0:T(8,128)} %reduce-scatter.71.cloned.1.call-done) | copy-start | bytes 4718596
  927.7 54.1 %copy-start.18 = (f32[256,384]{1,0:T(8,128)S(1)}, f32[256,384]{1,0:T(8,128)}, u32[]{:S(2)}) copy-start(f32[256,384]{1,0:T(8,128)} %copy-done.17) | copy-start | bytes 1179652
  927.7 54.1 %copy-start.91 = (f32[384]{0:T(512)S(1)}, f32[384]{0:T(512)}, u32[]{:S(2)}) copy-start(f32[384]{0:T(512)} %param.38) | copy-start | bytes 4612
  927.7 54.1 %copy-start.94 = (f32[256]{0:T(256)S(1)}, f32[256]{0:T(256)}, u32[]{:S(2)}) copy-start(f32[256]{0:T(256)} %copy-done.93) | copy-start | bytes 3076
  927.7 54.0 %copy-start.96 = (f32[256]{0:T(256)S(1)}, f32[256]{0:T(256)}, u32[]{:S(2)}) copy-start(f32[256]{0:T(256)} %copy-done.95) | copy-start | bytes 3076
  927.7 60.7 %copy-start.58 = (bf16[256,384]{1,0:T(8,128)(2,1)S(1)}, bf16[256,384]{1,0:T(8,128)(2,1)}, u32[]{:S(2)}) copy-start(bf16[256,384]{1,0:T(8,128)(2,1)} %reduce-scatter.65.cloned.1.call-done) | copy-start | bytes 589828
  927.7 54.0 %reduce-scatter.75.cloned.1.call-start = ((), (), s32[]{:S(2)}) async-start(), calls=%async_computation.56 | async-start | bytes 983040 | tf_op jit(solution)/shard_map/reduce_scatter | solution.py:56
  958.3 60.6 %reduce-scatter.77.cloned.1.call-start = ((), (), s32[]{:S(2)}) async-start(), calls=%async_computation.57 | async-start | bytes 1179648 | tf_op jit(solution)/shard_map/reduce_scatter | solution.py:55
  1000.2 53.0 %reduce-scatter.43.cloned.1.call-start = ((), (), s32[]{:S(2)}) async-start(), calls=%async_computation.36 | async-start | bytes 2621440 | tf_op jit(solution)/shard_map/reduce_scatter | solution.py:56
  1009.2 59.9 %reduce-scatter.81.cloned.1.call-start = ((), (), s32[]{:S(2)}) async-start(), calls=%async_computation.59 | async-start | bytes 589824 | tf_op jit(solution)/shard_map/reduce_scatter | solution.py:106
  1051.9 33.1 %reduce-scatter.79.cloned.1.call-start = ((), (), s32[]{:S(2)}) async-start(), calls=%async_computation.58 | async-start | bytes 589824 | tf_op jit(solution)/shard_map/reduce_scatter | solution.py:106
  1052.8 57.0 %all-gather.11.cloned.1.call-start = ((), (), s32[]{:S(2)}) async-start(), calls=%async_computation.37 | async-start | bytes 2621440 | tf_op jit(solution)/shard_map/all_gather | solution.py:22
  1057.3 77.3 %all-gather.23.cloned.1.call-start = ((), (), s32[]{:S(2)}) async-start(), calls=%async_computation.63 | async-start | bytes 2621440 | tf_op jit(solution)/shard_map/all_gather | solution.py:22
  1058.1 101.3 %all-gather.19.cloned.1.call-start = ((), (), s32[]{:S(2)}) async-start(), calls=%async_computation.60 | async-start | bytes 1769472 | tf_op jit(solution)/shard_map/all_gather | solution.py:26
  1058.1 51.7 %copy-start.56 = (bf16[1024,128]{1,0:T(8,128)(2,1)S(1)}, bf16[1024,128]{1,0:T(8,128)(2,1)}, u32[]{:S(2)}) copy-start(bf16[1024,128]{1,0:T(8,128)(2,1)} %param.50) | copy-start | bytes 786436
  1087.0 101.8 %all-gather.21.cloned.1.call-start = ((), (), s32[]{:S(2)}) async-start(), calls=%async_computation.62 | async-start | bytes 2359296 | tf_op jit(solution)/shard_map/all_gather | solution.py:26
  1087.7 130.5 %reduce-scatter.45.cloned.1.call-start = ((), (), s32[]{:S(2)}) async-start(), calls=%async_computation.38 | async-start | bytes 786432 | tf_op jit(solution)/shard_map/reduce_scatter | solution.py:55
  1113.0 119.9 %reduce-scatter.83.cloned.1.call-start = ((), (), s32[]{:S(2)}) async-start(), calls=%async_computation.61 | async-start | bytes 983040 | tf_op jit(solution)/shard_map/reduce_scatter | solution.py:56
  1114.2 45.2 %copy-start.49 = (bf16[384,3,192]{0,2,1:T(8,128)(2,1)S(1)}, bf16[384,3,192]{0,2,1:T(8,128)(2,1)}, u32[]{:S(2)}) copy-start(bf16[384,3,192]{0,2,1:T(8,128)(2,1)} %param.36) | copy-start | bytes 1327108
  1162.5 183.7 %all-reduce.13.cloned.1.call-start = ((), (), s32[]{:S(2)}) async-start(), calls=%async_computation.64 | async-start | bytes 5308416 | tf_op jit(solution)/shard_map/psum | solution.py:434
  1196.5 36.4 %copy-start.2 = (f32[256,384]{1,0:T(8,128)S(1)}, f32[256,384]{1,0:T(8,128)}, u32[]{:S(2)}) copy-start(f32[256,384]{1,0:T(8,128)} %copy-done.1) | copy-start | bytes 1179652
  1196.5 37.6 %copy-start.104 = (f32[384]{0:T(512)S(1)}, f32[384]{0:T(512)}, u32[]{:S(2)}) copy-start(f32[384]{0:T(512)} %get-tuple-element.632) | copy-start | bytes 4612
  1196.5 37.6 %copy-start.105 = (f32[384]{0:T(512)S(1)}, f32[384]{0:T(512)}, u32[]{:S(2)}) copy-start(f32[384]{0:T(512)} %get-tuple-element.660) | copy-start | bytes 4612
  1196.5 77.6 %copy-start.51 = (f32[256,384]{1,0:T(8,128)S(1)}, f32[256,384]{1,0:T(8,128)}, u32[]{:S(2)}) copy-start(f32[256,384]{1,0:T(8,128)} %get-tuple-element.818) | copy-start | bytes 1179652
  (99 other events, 1448.8 us)
Sparse Core Ops, SparseCore 0:
  28.2 35.0 reduce-scatter.28
  65.6 43.1 reduce-scatter.66
  111.8 23.2 reduce-scatter.30
  141.3 23.2 reduce-scatter.68
  182.8 44.5 reduce-scatter.32
  232.7 27.1 all-gather.8
  263.4 23.2 reduce-scatter.34
  298.9 14.9 reduce-scatter.36
  331.4 27.2 reduce-scatter.46
  397.0 14.9 reduce-scatter.48
  428.8 30.5 reduce-scatter.50
  461.8 31.4 reduce-scatter.52
  496.1 22.5 all-gather.12
  521.9 14.5 reduce-scatter.54
  555.6 20.7 reduce-scatter.56
  616.7 21.6 reduce-scatter.60
  641.3 21.6 reduce-scatter.58
  665.0 19.8 all-gather.14
  687.8 14.5 reduce-scatter.62
  712.2 28.1 reduce-scatter.38
  778.8 14.9 reduce-scatter.40
  810.7 22.3 reduce-scatter.64
  835.4 43.3 reduce-scatter.70
  880.9 43.3 reduce-scatter.72
  927.8 27.2 all-gather.16
  958.5 23.2 reduce-scatter.74
  1000.3 18.6 reduce-scatter.76
  1021.6 31.5 reduce-scatter.42
  1056.0 13.1 reduce-scatter.80
  1071.9 13.1 reduce-scatter.78
  1087.2 22.5 all-gather.10
  1112.0 22.5 all-gather.22
  1136.6 22.7 all-gather.18
  1161.5 27.2 all-gather.20
  1191.6 14.7 reduce-scatter.44
  1209.5 23.3 reduce-scatter.82
  1237.6 108.6 all-reduce.12
where the time goes:
time: 1380 us; the launch traced here: 1370 us
  waiting for transfers between devices  772 us (56%)
  blocking collectives  298 us (22%)
  matrix products  111 us (8%)
  other arithmetic  94.8 us (7%)
  local copies, waits for them, and re-layouts  61.4 us (4%)
  between operations  16.4 us (1%)
    reduce_scatter x12, waiting for transfers between devices, sum_features(): lax.psum_scatter(partial_term(), 'row', scatter_dimension=0, tiled=True)  227 us
    reduce_scatter x12, waiting for transfers between devices, sum_features(): lax.psum_scatter(partial_term().astype(jnp.bfloat16), 'col', scatter_dime...  220 us
    all_gather x4, waiting for transfers between devices, collect_row(): return lax.all_gather(values, 'row', axis=0, tiled=True)  97.1 us
    all_gather x4, waiting for transfers between devices, collect_col(): return lax.all_gather(values, 'col', axis=0, tiled=True)  85.2 us
    all_gather x9, blocking collectives, collect_col(): return lax.all_gather(values, 'col', axis=0, tiled=True)  72.1 us
    psum x1, waiting for transfers between devices, per_device(): lax.psum(decoder_grads[2].astype(jnp.bfloat16), 'dp').astype(jnp.float32)  70.3 us
    all_gather x9, blocking collectives, collect_row(): return lax.all_gather(values, 'row', axis=0, tiled=True)  58.8 us
    reduce_scatter x2, waiting for transfers between devices, key_sum(): lax.psum_scatter(as_sent(kv_pair), 'col', scatter_dimension=0, tiled=True)  44.4 us
  transfers between devices with their start and end apart: 37, of which 35 were waited for; matrix products, arithmetic and copies ran while one was open for 8% of the time, Pallas kernels for 0%

commit v1 on v0

v1 whole, which is shorter than its diff:
```python
import functools

import jax
import jax.numpy as jnp
from jax import lax
from jax.experimental import pallas as pl
from jax.experimental.pallas import tpu as pltpu
from jax.sharding import Mesh, PartitionSpec as P

D1 = 768
D2 = 512
HD1 = 64
HD2 = 32
EPSILON = 1e-06
BLOCK = 512
LANES = 128
LOG2E = 1.4426950408889634
SWAP = [(0, 1), (1, 0)]
BF16 = jnp.bfloat16
F32 = jnp.float32


def mm(left, right):
    return jnp.dot(left, right, preferred_element_type=F32)


def mm_nt(left, right):
    return lax.dot_general(left, right, (((1,), (1,)), ((), ())), preferred_element_type=F32)


def mm_tn(left, right):
    return lax.dot_general(left, right, (((0,), (0,)), ((), ())), preferred_element_type=F32)


def swap(value, axis):
    return lax.ppermute(value, axis, SWAP)


def gather_four(block):
    half = block.shape[0] // 2
    by_x = swap(block, "row")
    by_y = swap(block, "y")
    first = swap(by_x[:half], "y")
    second = swap(by_y[half:], "row")
    return (block, by_x, by_y, jnp.concatenate([first, second], 0))


def head_lanes(head, head_size, rows):
    lane = lax.broadcasted_iota(jnp.int32, (rows, LANES), 1)
    return (lane >= head * head_size) & (lane < (head + 1) * head_size)


def attention_forward_kernel(head_size, q_ref, k_ref, v_ref, limit_ref, out_ref, inv_ref, aug_ref):
    tile = pl.program_id(1)
    rows = q_ref.shape[0]
    heads = LANES // head_size
    per_block = BLOCK // rows
    scale = head_size ** (-0.5) * LOG2E

    @pl.when(tile == 0)
    def _():
        aug_ref[:, :LANES] = v_ref[...]
        aug_ref[:, LANES:] = jnp.ones_like(v_ref)

    def run(block):
        queries = q_ref[...]
        limits = limit_ref[...]
        places = block * BLOCK + lax.broadcasted_iota(jnp.int32, (rows, BLOCK), 1)
        visible = places <= limits
        result = jnp.zeros((rows, LANES), F32)
        inverses = jnp.zeros((rows, LANES), F32)
        for head in range(heads):
            own = head_lanes(head, head_size, rows)
            masked = jnp.where(own, queries, jnp.zeros_like(queries))
            total = jnp.zeros((rows, 2 * LANES), F32)
            for part in range(block + 1):
                span = slice(part * BLOCK, (part + 1) * BLOCK)
                weights = jnp.exp2(mm_nt(masked, k_ref[span, :]) * scale)
                if part == block:
                    weights = jnp.where(visible, weights, 0.0)
                total = total + mm(weights.astype(BF16), aug_ref[span, :])
            inverse = 1.0 / total[:, LANES:]
            result = jnp.where(own, total[:, :LANES] * inverse, result)
            inverses = jnp.where(own, inverse, inverses)
        out_ref[...] = result.astype(BF16)
        inv_ref[...] = inverses

    for block in range(k_ref.shape[0] // BLOCK):
        pl.when(tile // per_block == block)(functools.partial(run, block))


def attention_forward(mixed, limits, head_size):
    length, width = mixed.shape[0], mixed.shape[1] // 3
    groups = width // LANES
    rows = 256
    return pl.pallas_call(
        functools.partial(attention_forward_kernel, head_size),
        out_shape=(
            jax.ShapeDtypeStruct((length, width), BF16),
            jax.ShapeDtypeStruct((length, width), F32),
        ),
        grid=(groups, length // rows),
        in_specs=[
            pl.BlockSpec((rows, LANES), lambda g, t: (t, g)),
            pl.BlockSpec((length, LANES), lambda g, t: (0, groups + g)),
            pl.BlockSpec((length, LANES), lambda g, t: (0, 2 * groups + g)),
            pl.BlockSpec((rows, 1), lambda g, t: (t, 0)),
        ],
        out_specs=[
            pl.BlockSpec((rows, LANES), lambda g, t: (t, g)),
            pl.BlockSpec((rows, LANES), lambda g, t: (t, g)),
        ],
        scratch_shapes=[pltpu.VMEM((length, 2 * LANES), BF16)],
        compiler_params=pltpu.CompilerParams(vmem_limit_bytes=40 << 20),
        name="attention_forward",
    )(mixed, mixed, mixed, limits)


def attention_backward_kernel(
    head_size,
    pairs,
    q_ref,
    k_ref,
    v_ref,
    att_ref,
    inv_ref,
    grad_ref,
    limit_ref,
    dq_ref,
    dk_ref,
    dv_ref,
    vaug_ref,
    naug_ref,
    dq_acc,
    dk_acc,
    dv_acc,
):
    step = pl.program_id(1)
    length = q_ref.shape[0]
    heads = LANES // head_size
    scaling = head_size ** (-0.5)

    @pl.when(step == 0)
    def _():
        lane = lax.broadcasted_iota(jnp.int32, (length, LANES), 1)
        vaug_ref[:, :LANES] = v_ref[...]
        vaug_ref[:, LANES:] = jnp.where(lane < 2, 1.0, 0.0).astype(BF16)
        scaled = grad_ref[...] * inv_ref[...]
        terms = scaled * att_ref[...].astype(F32)
        low = scaled.astype(BF16)
        for head in range(heads):
            own = head_lanes(head, head_size, length)
            total = -jnp.sum(jnp.where(own, terms, 0.0), 1, keepdims=True)
            high = total.astype(BF16).astype(F32)
            rest = total - high
            naug_ref[head, :, :LANES] = jnp.where(own, low, jnp.zeros_like(low))
            naug_ref[head, :, LANES:] = jnp.where(
                lane == 0, high, jnp.where(lane == 1, rest, 0.0)
            ).astype(BF16)
        dq_acc[...] = jnp.zeros_like(dq_acc)
        dk_acc[...] = jnp.zeros_like(dk_acc)
        dv_acc[...] = jnp.zeros_like(dv_acc)

    def run(key_block, query_block):
        keys = slice(key_block * BLOCK, (key_block + 1) * BLOCK)
        queries = slice(query_block * BLOCK, (query_block + 1) * BLOCK)
        key_rows = k_ref[keys, :]
        query_rows = q_ref[queries, :]
        key_flipped = key_rows.astype(F32).T.astype(BF16)
        if key_block == query_block:
            places = key_block * BLOCK + lax.broadcasted_iota(jnp.int32, (BLOCK, BLOCK), 0)
            visible = places <= limit_ref[:, queries]
        dq = jnp.zeros((LANES, BLOCK), F32)
        dk = jnp.zeros((BLOCK, LANES), F32)
        dv = jnp.zeros((BLOCK, LANES), F32)
        for head in range(heads):
            own = head_lanes(head, head_size, BLOCK)
            masked = jnp.where(own, query_rows, jnp.zeros_like(query_rows))
            weights = jnp.exp2(mm_nt(key_rows, masked) * (scaling * LOG2E))
            if key_block == query_block:
                weights = jnp.where(visible, weights, 0.0)
            naug = naug_ref[head, queries, :]
            slopes = mm_nt(vaug_ref[keys, :], naug)
            scores = (weights * slopes).astype(BF16)
            dv += mm(weights.astype(BF16), naug[:, :LANES])
            dk += mm(scores, masked)
            row = lax.broadcasted_iota(jnp.int32, (LANES, BLOCK), 0)
            mine = (row >= head * head_size) & (row < (head + 1) * head_size)
            dq += mm(jnp.where(mine, key_flipped, jnp.zeros_like(key_flipped)), scores)
        dq_acc[:, queries] += dq
        dk_acc[keys, :] += dk
        dv_acc[keys, :] += dv

    for number, (key_block, query_block) in enumerate(pairs):
        pl.when(step == number)(functools.partial(run, key_block, query_block))

    @pl.when(step == len(pairs) - 1)
    def _():
        dq_ref[...] = (dq_acc[...].T * scaling).astype(BF16)
        dk_ref[...] = (dk_acc[...] * scaling).astype(BF16)
        dv_ref[...] = dv_acc[...].astype(BF16)


def attention_backward(mixed, attended, inverse, grad, limits_row, head_size):
    length, width = attended.shape
    groups = width // LANES
    blocks = length // BLOCK
    pairs = [(k, q) for q in range(blocks) for k in range(q + 1)]
    whole = lambda offset: pl.BlockSpec((length, LANES), lambda g, s: (0, offset + g))
    return pl.pallas_call(
        functools.partial(attention_backward_kernel, head_size, pairs),
        out_shape=(jax.ShapeDtypeStruct((length, width), BF16),) * 3,
        grid=(groups, len(pairs)),
        in_specs=[
            whole(0),
            whole(groups),
            whole(2 * groups),
            whole(0),
            whole(0),
            whole(0),
            pl.BlockSpec((1, length), lambda g, s: (0, 0)),
        ],
        out_specs=[whole(0), whole(0), whole(0)],
        scratch_shapes=[
            pltpu.VMEM((length, 2 * LANES), BF16),
            pltpu.VMEM((LANES // head_size, length, 2 * LANES), BF16),
            pltpu.VMEM((LANES, length), F32),
            pltpu.VMEM((length, LANES), F32),
            pltpu.VMEM((length, LANES), F32),
        ],
        compiler_params=pltpu.CompilerParams(vmem_limit_bytes=40 << 20),
        name="attention_backward",
    )(mixed, mixed, mixed, attended, inverse, grad, limits_row)


def norm_stats(values):
    width = values.shape[1]
    average = jnp.sum(values, 1, keepdims=True) / width
    variance = jnp.sum(values * values, 1, keepdims=True) / width - average * average
    inverse = lax.rsqrt(variance + EPSILON)
    return ((values - average) * inverse, inverse)


def norm_backward(incoming, centred, inverse, gain):
    width = incoming.shape[1]
    scaled = incoming * gain
    first = jnp.sum(scaled, 1, keepdims=True) / width
    second = jnp.sum(scaled * centred, 1, keepdims=True) / width
    return inverse * (scaled - first - centred * second)


def gelu_pair(values):
    area = 0.5 * (1.0 + lax.erf(values * (0.5**0.5)))
    slope = area + values * jnp.exp(-0.5 * values * values) * (0.5 / jnp.pi) ** 0.5
    return (values * area, slope)


def core_sum(partial):
    low = partial.astype(BF16)
    return low.astype(F32) + swap(low, "core").astype(F32)


def dp_sum(value, size):
    if size & (size - 1):
        return lax.psum(value, "dp")
    distance = 1
    while distance < size:
        pairs = [(i, i ^ distance) for i in range(size)]
        value = value + lax.ppermute(value, "dp", pairs)
        distance *= 2
    return value


def block_forward(stream, params, limits, head_size):
    first_gain, first_bias, mixing, output, second_gain, second_bias, upward = params
    centred_first, inverse_first = norm_stats(stream)
    normed_first = (centred_first * first_gain + first_bias).astype(BF16)
    mixed = mm(normed_first, mixing).astype(BF16)
    attended, inverse = attention_forward(mixed, limits, head_size)
    middle = stream + core_sum(mm(attended, output))
    centred_second, inverse_second = norm_stats(middle)
    normed_second = (centred_second * second_gain + second_bias).astype(BF16)
    hidden = mm(normed_second, upward)
    active, slope = gelu_pair(hidden)
    kept = (
        centred_first,
        inverse_first,
        normed_first,
        mixed,
        attended,
        inverse,
        centred_second,
        inverse_second,
        normed_second,
        slope.astype(BF16),
    )
    return (middle, active.astype(BF16), kept)


def block_backward(out_grad, params, downward, kept, limits_row, head_size):
    first_gain, first_bias, mixing, output, second_gain, second_bias, upward = params
    (
        centred_first,
        inverse_first,
        normed_first,
        mixed,
        attended,
        inverse,
        centred_second,
        inverse_second,
        normed_second,
        slope,
    ) = kept
    down_low = out_grad.astype(BF16)
    hidden_low = (mm_nt(down_low, downward) * slope.astype(F32)).astype(BF16)
    second_grad = core_sum(mm_nt(hidden_low, upward))
    middle_grad = out_grad + norm_backward(second_grad, centred_second, inverse_second, second_gain)
    middle_low = middle_grad.astype(BF16)
    attended_grad = mm_nt(middle_low, output)
    mixed_low = jnp.concatenate(
        attention_backward(mixed, attended, inverse, attended_grad, limits_row, head_size), 1
    )
    return (down_low, hidden_low, second_grad, middle_grad, middle_low, mixed_low)


def per_device(
    data_size,
    block_input,
    span_end,
    encoder_attention_gain,
    encoder_attention_bias,
    encoder_query_key_value,
    encoder_output_weight,
    encoder_feedforward_gain,
    encoder_feedforward_bias,
    encoder_up_weight,
    encoder_down_weight,
    projection,
    decoder_attention_gain,
    decoder_attention_bias,
    decoder_query_key_value,
    decoder_output_weight,
    decoder_feedforward_gain,
    decoder_feedforward_bias,
    decoder_up_weight,
    decoder_down_weight,
    output_cotangent,
):
    row = lax.axis_index("row")
    y = lax.axis_index("y")
    core = lax.axis_index("core")
    length = span_end.shape[0]
    own_rows = block_input.shape[0]
    limits = span_end.reshape(length, 1)
    limits_row = span_end.reshape(1, length)

    parts = gather_four(block_input)
    near = jnp.concatenate([parts[0], parts[1]], 1)
    far = jnp.concatenate([parts[2], parts[3]], 1)
    sides = lax.all_gather(
        jnp.stack([near, far]), "core", axis=1, tiled=False
    )
    ordered = jnp.where(y == 0, sides, sides[::-1])
    encoder_in = ordered.reshape(length, -1)

    vectors = jnp.stack(
        [
            encoder_attention_gain,
            encoder_attention_bias,
            encoder_feedforward_gain,
            encoder_feedforward_bias,
        ]
    )
    encoder_vectors = jnp.concatenate([vectors, swap(vectors, "row")], 1)
    vectors = jnp.stack(
        [
            decoder_attention_gain,
            decoder_attention_bias,
            decoder_feedforward_gain,
            decoder_feedforward_bias,
        ]
    )
    vectors = lax.all_gather(vectors, "core", axis=1, tiled=True)
    decoder_vectors = jnp.concatenate([vectors, swap(vectors, "y")], 1)

    def square(parts, row_dim):
        own, by_x, by_y, by_both = parts
        if row_dim == 0:
            return jnp.concatenate(
                [jnp.concatenate([own, by_y], 1), jnp.concatenate([by_x, by_both], 1)], 0
            )
        return jnp.concatenate(
            [jnp.concatenate([own, by_x], 1), jnp.concatenate([by_y, by_both], 1)], 0
        )

    def mixing_square(parts, row_dim):
        width = parts[0].shape[1] // 3
        return jnp.concatenate(
            [square([p[:, i * width : (i + 1) * width] for p in parts], row_dim) for i in range(3)],
            1,
        )

    mixing = encoder_query_key_value.reshape(encoder_query_key_value.shape[0], -1)
    encoder_mixing = mixing_square(gather_four(mixing), 0)
    encoder_output = square(gather_four(encoder_output_weight), 1)
    encoder_up = square(gather_four(encoder_up_weight), 0)
    encoder_down = square(gather_four(encoder_down_weight), 1)
    pieces = square(gather_four(projection), 0)
    both = lax.all_gather(pieces, "core", axis=0, tiled=False)
    width = projection.shape[1]
    projection_all = jnp.concatenate(
        [both[0, :, :width], both[1, :, :width], both[0, :, width:], both[1, :, width:]], 1
    )

    def core_rows(value):
        return lax.all_to_all(value, "core", value.ndim - 1, 0, tiled=True)

    def core_columns(value):
        return lax.all_to_all(value, "core", 0, value.ndim - 1, tiled=True)

    mixing = core_rows(decoder_query_key_value)
    mixing = mixing.reshape(mixing.shape[0], -1)
    decoder_mixing = mixing_square(gather_four(mixing), 1)
    decoder_output = square(gather_four(core_columns(decoder_output_weight)), 0)
    decoder_up = square(gather_four(core_rows(decoder_up_weight)), 1)
    decoder_down = square(gather_four(core_columns(decoder_down_weight)), 0)

    cotangent = lax.all_gather(output_cotangent, "core", axis=1, tiled=True)
    cotangent = jnp.concatenate([cotangent, swap(cotangent, "y")], 1)
    other = swap(cotangent, "row")
    cotangent = jnp.where(
        row == 0,
        jnp.concatenate([cotangent, other], 0),
        jnp.concatenate([other, cotangent], 0),
    )

    encoder_params = (
        encoder_vectors[0],
        encoder_vectors[1],
        encoder_mixing,
        encoder_output,
        encoder_vectors[2],
        encoder_vectors[3],
        encoder_up,
    )
    decoder_params = (
        decoder_vectors[0],
        decoder_vectors[1],
        decoder_mixing,
        decoder_output,
        decoder_vectors[2],
        decoder_vectors[3],
        decoder_up,
    )

    stream = encoder_in.astype(F32)
    middle, encoder_active, encoder_kept = block_forward(stream, encoder_params, limits, HD1)
    encoder_out = middle + core_sum(mm(encoder_active, encoder_down))
    encoder_low = encoder_out.astype(BF16)
    decoder_in = mm(encoder_low, projection_all)
    decoder_middle, decoder_active, decoder_kept = block_forward(
        decoder_in, decoder_params, limits, HD2
    )
    own_tokens = (2 * y + core) * own_rows
    own_encoder_out = lax.dynamic_slice(
        encoder_out, (own_tokens, 0), (own_rows, block_input.shape[1])
    )
    out_rows, out_columns = output_cotangent.shape
    active_rows = lax.dynamic_slice_in_dim(decoder_active, row * out_rows, out_rows, 0)
    last = mm(active_rows, decoder_down[:, : 2 * out_columns])
    mine = lax.dynamic_slice_in_dim(last, core * out_columns, out_columns, 1)
    others = lax.dynamic_slice_in_dim(last, (1 - core) * out_columns, out_columns, 1)
    own_decoder_out = (
        lax.dynamic_slice(
            decoder_middle, (row * out_rows, core * out_columns), (out_rows, out_columns)
        )
        + mine
        + swap(others.astype(BF16), "core").astype(F32)
    )

    down_low, hidden_low, second_grad, middle_grad, middle_low, mixed_low = block_backward(
        cotangent.astype(F32), decoder_params, decoder_down, decoder_kept, limits_row, HD2
    )
    first_grad = core_sum(mm_nt(mixed_low, decoder_mixing))
    decoder_grad = middle_grad + norm_backward(
        first_grad, decoder_kept[0], decoder_kept[1], decoder_vectors[0]
    )

    def own_sums(first_grad, second_grad, kept):
        def part(value):
            return lax.dynamic_slice_in_dim(value, own_tokens, own_rows, 0)

        first, second = part(first_grad), part(second_grad)
        return jnp.stack(
            [
                jnp.sum(first * part(kept[0]), 0),
                jnp.sum(first, 0),
                jnp.sum(second * part(kept[6]), 0),
                jnp.sum(second, 0),
            ]
        )

    decoder_sums = own_sums(first_grad, second_grad, decoder_kept)
    heads_own = decoder_query_key_value.shape[2] // 2
    features = 2 * decoder_output_weight.shape[1]
    columns = mixed_low.shape[1] // 3
    mixed_own = jnp.concatenate(
        [mixed_low[:, i * columns : i * columns + heads_own] for i in range(3)], 1
    )
    units = decoder_up_weight.shape[1] // 2
    decoder_weight_grads = [
        mm_tn(decoder_kept[2][:, :features], mixed_own).astype(BF16),
        mm_tn(decoder_kept[4][:, :heads_own], middle_low[:, :features]).astype(BF16),
        mm_tn(decoder_kept[8][:, :features], hidden_low[:, :units]).astype(BF16),
        mm_tn(decoder_active[:, :units], down_low[:, :features]).astype(BF16),
    ]

    projection_low = decoder_grad.astype(BF16)
    projection_own = lax.dynamic_slice_in_dim(
        projection_low, core * projection.shape[1], projection.shape[1], 1
    )
    projection_grad = mm_tn(encoder_low[:, : projection.shape[0]], projection_own).astype(BF16)
    encoder_grad = mm_nt(projection_low, projection_all)

    down_low, hidden_low, second_grad, middle_grad, middle_low, mixed_low = block_backward(
        encoder_grad, encoder_params, encoder_down, encoder_kept, limits_row, HD1
    )
    first_grad = core_sum(mm_nt(mixed_low, encoder_mixing))
    input_grad = middle_grad + norm_backward(
        first_grad, encoder_kept[0], encoder_kept[1], encoder_vectors[0]
    )
    own_input_grad = lax.dynamic_slice(
        input_grad, (own_tokens, 0), (own_rows, block_input.shape[1])
    )
    encoder_sums = own_sums(first_grad, second_grad, encoder_kept)
    features = encoder_up_weight.shape[0]
    heads_own = encoder_output_weight.shape[0]
    columns = mixed_low.shape[1] // 3
    mixed_own = jnp.concatenate(
        [mixed_low[:, i * columns : i * columns + heads_own] for i in range(3)], 1
    )
    units = encoder_up_weight.shape[1]
    encoder_weight_grads = [
        mm_tn(encoder_kept[2][:, :features], mixed_own).astype(BF16),
        mm_tn(encoder_kept[4][:, :heads_own], middle_low[:, :features]).astype(BF16),
        mm_tn(encoder_kept[8][:, :features], hidden_low[:, :units]).astype(BF16),
        mm_tn(encoder_active[:, :units], down_low[:, :features]).astype(BF16),
    ]

    decoder_weight_grads = [dp_sum(g, data_size).astype(F32) for g in decoder_weight_grads]
    projection_grad = dp_sum(projection_grad, data_size).astype(F32)
    encoder_weight_grads = [dp_sum(g, data_size).astype(F32) for g in encoder_weight_grads]
    encoder_sums = lax.psum(encoder_sums[:, :features], ("dp", "y", "core"))
    decoder_sums = jnp.where(
        y == 0,
        decoder_sums,
        jnp.concatenate(
            [decoder_sums[:, decoder_sums.shape[1] // 2 :], decoder_sums[:, : decoder_sums.shape[1] // 2]], 1
        ),
    )
    decoder_sums = lax.psum(decoder_sums, ("dp", "y", "core"))
    share = decoder_attention_gain.shape[0]
    decoder_sums = lax.dynamic_slice_in_dim(decoder_sums, (2 * y + core) * share, share, 1)

    decoder_weight_grads = [
        core_columns(
            decoder_weight_grads[0].reshape(decoder_weight_grads[0].shape[0], 3, -1)
        ),
        core_rows(decoder_weight_grads[1]),
        core_columns(decoder_weight_grads[2]),
        core_rows(decoder_weight_grads[3]),
    ]
    return (
        own_encoder_out,
        own_decoder_out,
        own_input_grad,
        encoder_sums[0],
        encoder_sums[1],
        encoder_weight_grads[0].reshape(encoder_query_key_value.shape),
        encoder_weight_grads[1],
        encoder_sums[2],
        encoder_sums[3],
        encoder_weight_grads[2],
        encoder_weight_grads[3],
        projection_grad,
        decoder_sums[0],
        decoder_sums[1],
        decoder_weight_grads[0],
        decoder_weight_grads[1],
        decoder_sums[2],
        decoder_sums[3],
        decoder_weight_grads[2],
        decoder_weight_grads[3],
    )


def solution(mesh):
    data, row, col = (mesh.shape[name] for name in ("dp", "row", "col"))
    split = Mesh(mesh.devices.reshape(data, row, col // 2, 2), ("dp", "row", "y", "core"))
    c = ("y", "core")
    in_specs = (
        P(("dp", *c), "row"),
        P("dp"),
        P("row"),
        P("row"),
        P("row", None, c),
        P(c, "row"),
        P("row"),
        P("row"),
        P("row", c),
        P(c, "row"),
        P("row", c),
        P(c),
        P(c),
        P(c, None, "row"),
        P("row", c),
        P(c),
        P(c),
        P(c, "row"),
        P("row", c),
        P(("dp", "row"), c),
    )
    out_specs = (
        P(("dp", *c), "row"),
        P(("dp", "row"), c),
        P(("dp", *c), "row"),
        P("row"),
        P("row"),
        P("row", None, c),
        P(c, "row"),
        P("row"),
        P("row"),
        P("row", c),
        P(c, "row"),
        P("row", c),
        P(c),
        P(c),
        P(c, None, "row"),
        P("row", c),
        P(c),
        P(c),
        P(c, "row"),
        P("row", c),
    )
    return jax.shard_map(
        functools.partial(per_device, data),
        mesh=split,
        in_specs=in_specs,
        out_specs=out_specs,
        check_vma=False,
    )
```

time: 1380 us -> 589 us (0.43)
  waiting for transfers between devices: 772 us -> 105 us
  blocking collectives: 298 us -> 93.1 us
  starting transfers between devices: 2.62 us -> 81.2 us
  Pallas kernels: 0 us -> 58 us
  matrix products: 111 us -> 81.5 us
    reduce_scatter x28 -> x0, waiting for transfers between devices: 518 us -> none  [the longest x12 227 us: sum_features(): lax.psum_scatter(partial_term(), 'row', scatter_dimension=0, tiled=True)]
    all_gather x26 -> x3, blocking collectives: 192 us -> 7.13 us  [the longest x1 2.98 us: per_device(): cotangent = lax.all_gather(output_cotangent, 'core', axis=1, tiled=True)]
    all_gather x8 -> x1, waiting for transfers between devices: 182 us -> 0.01 us  [per_device(): sides = lax.all_gather(jnp.stack([near, far]), 'core', axis=1, tiled=False)]
    ppermute x0 -> x70, waiting for transfers between devices: none -> 104 us  [the longest x18 62.8 us: dp_sum(): value = value + lax.ppermute(value, 'dp', pairs)]
    ppermute x0 -> x70, starting transfers between devices: none -> 74.5 us  [the longest x52 52.4 us: swap(): return lax.ppermute(value, axis, SWAP)]
    psum x1 -> x0, waiting for transfers between devices: 70.3 us -> none  [per_device(): lax.psum(decoder_grads[2].astype(jnp.bfloat16), 'dp').astype(jnp.float32)]
    pallas_call x0 -> x4, Pallas kernels: none -> 58 us  [the longest x2 36.5 us: attention_backward(): pl.pallas_call(functools.partial(attention_backward_kernel, head_size, pa...]
    psum x10 -> x1, blocking collectives: 106 us -> 59.6 us  [per_device(): encoder_sums = lax.psum(encoder_sums[:, :features], ('dp', 'y', 'core'))]
  transfers between devices with their start and end apart: 37 -> 73, of which waited for: 35 -> 17; matrix products, arithmetic and copies ran while one was open for 8% -> 34% of each run, Pallas kernels for 0% -> 10%
where the time goes in v1:
time: 589 us; the launch traced here: 577 us
  waiting for transfers between devices  105 us (18%)
  blocking collectives  93.1 us (16%)
  other arithmetic  87.1 us (15%)
  matrix products  81.5 us (14%)
  starting transfers between devices  81.2 us (14%)
  Pallas kernels  58 us (10%)
  local copies, waits for them, and re-layouts  54.4 us (9%)
  between operations  16.9 us (3%)
    ppermute x18, waiting for transfers between devices, dp_sum(): value = value + lax.ppermute(value, 'dp', pairs)  62.8 us
    psum x1, blocking collectives, per_device(): encoder_sums = lax.psum(encoder_sums[:, :features], ('dp', 'y', 'core'))  59.6 us
    ppermute x52, starting transfers between devices, swap(): return lax.ppermute(value, axis, SWAP)  52.4 us
    ppermute x52, waiting for transfers between devices, swap(): return lax.ppermute(value, axis, SWAP)  41.7 us
    dot_general x9, matrix products, mm_nt(): lax.dot_general(left, right, (((1,), (1,)), ((), ())), preferred_element_...  36.9 us
    pallas_call x2, Pallas kernels, attention_backward(): pl.pallas_call(functools.partial(attention_backward_kernel, head_size, pa...  36.5 us
    dot_general x9, matrix products, mm(): return jnp.dot(left, right, preferred_element_type=F32)  29 us
    ppermute x18, starting transfers between devices, dp_sum(): value = value + lax.ppermute(value, 'dp', pairs)  22 us
  transfers between devices with their start and end apart: 73, of which 17 were waited for; matrix products, arithmetic and copies ran while one was open for 34% of the time, Pallas kernels for 10%

profile of v1, /device:TPU:0, one launch (start us, length us, event | category | flops | bytes accessed | tf_op | source)
XLA Modules:
  0.0 577.1 jit_solution(16677010186147633373)
XLA Ops:
  7.2 3.0 collective-permute-start.9
  25.3 9.8 %collective-permute-done.2 = bf16[128,384]{1,0:T(8,128)(2,1)S(1)} collective-permute-done((bf16[128,384]{1,0:T(8,128)(2,1)S(1)}, bf16[128,384]{1,0:T(8,128)(2,1)S(1)}, u32[]{:S(2)}, u32[]{:S(2)}) %collective-permute-start.2) | collective-permute-done | bytes 98336 | tf_op jit(solution)/shard_map/ppermute | solution.py:36
  40.1 3.2 collective-permute-done.7
  45.4 18.1 %fusion.24 = bf16[768,1152]{0,1:T(8,128)(2,1)} fusion(bf16[192,576]{0,1:T(8,128)(2,1)S(1)} %collective-permute-done.8, bf16[192,576]{0,1:T(8,128)(2,1)S(1)} %collective-permute-done.7, bf16[384,192]{0,1:T(8,128)(2,1)S(1)} %get-tuple-element.186, bf16[384,192]{0,1:T(8,128)(2,1)S(1)} %get-tuple-element.183, bf16[384,192]{0,1:T(8,128)(2,1)S(1)} %get-tuple-element.180, ...), kind=kLoop, calls=%fused_computation.67 | loop fusion | flops 29196288 | bytes 3833856 | tf_op jit(solution)/shard_map/concatenate | solution.py:398
  63.5 3.7 copy.107
  67.1 3.2 fusion.117
  70.4 3.3 fusion.28
  73.7 6.0 %reshape.215 = f32[1024,768]{0,1:T(8,128)} reshape(f32[2,2,256,768]{2,1,0,3:T(2,128)} %fusion.28) | data formatting | bytes 6291456 | tf_op jit(solution)/shard_map/convert_element_type | solution.py:456
  79.7 4.2 add_convert_fusion.1
  85.1 2.3 convolution_convert_fusion.q_ref.k_ref.v_ref
  87.4 10.8 %attention_forward.2 = (bf16[1024,384]{1,0:T(8,128)(2,1)S(1)}, f32[1024,384]{1,0:T(8,128)S(1)}) custom-call(bf16[1024,1152]{1,0:T(8,128)(2,1)S(1)} %convolution_convert_fusion.q_ref.k_ref.v_ref, bf16[1024,1152]{1,0:T(8,128)(2,1)S(1)} %convolution_convert_fusion.q_ref.k_ref.v_ref, bf16[1024,1152]{1,0:T(8,128)(2,1)S(1)} %convolution_convert_fusion.q_ref.k_ref.v_ref, ...), custom_call_target="tpu_custom_call" | custom-call | tf_op jit(solution)/shard_map/attention_forward/pallas_call | solution.py:96
  98.3 3.7 convolution_convert_fusion.2
  113.1 3.3 all-to-all-start.1
  118.2 3.4 all-to-all-start
  128.6 8.8 %collective-permute-done.18 = bf16[768,384]{1,0:T(8,128)(2,1)} collective-permute-done((bf16[768,384]{1,0:T(8,128)(2,1)}, bf16[768,384]{1,0:T(8,128)(2,1)}, u32[]{:S(2)}, u32[]{:S(2)}) %collective-permute-start.18) | collective-permute-done | bytes 589856 | tf_op jit(solution)/shard_map/ppermute | solution.py:36
  143.1 2.8 fusion.119
  145.9 2.2 add_convert_fusion
  150.6 9.0 %multiply_convert_fusion.1 = (bf16[1024,1536]{1,0:T(8,128)(2,1)S(1)}, f32[1024,1536]{1,0:T(8,128)}) fusion(bf16[1024,768]{0,1:T(8,128)(2,1)S(1)} %get-tuple-element.164, bf16[192,768]{1,0:T(8,128)(2,1)S(1)} %collective-permute-done.17, bf16[192,768]{1,0:T(8,128)(2,1)S(1)} %collective-permute-done.16, bf16[384,768]{1,0:T(8,128)(2,1)} %collective-permute-done.15, ...), kind=kOutput, calls=%fused_computation.8 | convolution fusion | flops 2435579904 | bytes 13369344 | tf_op jit(solution)/shard_map/dot_general | solution.py:24
  161.0 4.2 convolution_convert_fusion.4
  170.2 2.4 all-gather.1
  176.9 3.3 collective-permute-done.30
  180.4 2.6 fusion.123
  188.2 10.7 %attention_forward.3 = (bf16[1024,256]{1,0:T(8,128)(2,1)S(1)}, f32[1024,256]{1,0:T(8,128)S(1)}) custom-call(bf16[1024,768]{1,0:T(8,128)(2,1)S(1)} %convolution_convert_fusion.1.q_ref.k_ref.v_ref, bf16[1024,768]{1,0:T(8,128)(2,1)S(1)} %convolution_convert_fusion.1.q_ref.k_ref.v_ref, bf16[1024,768]{1,0:T(8,128)(2,1)S(1)} %convolution_convert_fusion.1.q_ref.k_ref.v_ref, ...), custom_call_target="tpu_custom_call" | custom-call | tf_op jit(solution)/shard_map/attention_forward/pallas_call | solution.py:96
  201.4 3.0 all_gather.23
  205.8 3.9 all_to_all.161
  216.1 5.8 %all_to_all.162 = bf16[2,512,128]{2,1,0:T(8,128)(2,1)} all-to-all(bf16[2,512,128]{2,1,0:T(8,128)(2,1)} %bitcast.132), channel_id=1, replica_groups=mesh['dp'=4,'row'=2,'y'=2,'core'=2] {'core'}, dimensions={0} | all-to-all | bytes 524288 | tf_op jit(solution)/shard_map/all_to_all | solution.py:419
  226.9 7.8 %collective-permute-done.37 = bf16[256,512]{1,0:T(8,128)(2,1)} collective-permute-done((bf16[256,512]{1,0:T(8,128)(2,1)}, bf16[256,512]{1,0:T(8,128)(2,1)}, u32[]{:S(2)}, u32[]{:S(2)}) %collective-permute-start.37) | collective-permute-done | bytes 262176 | tf_op jit(solution)/shard_map/ppermute | solution.py:36
  236.9 3.0 collective-permute-done.42
  246.8 2.6 fusion.120
  251.4 4.5 multiply_convert_fusion.3
  256.0 6.1 %multiply_convert_fusion.2 = bf16[1024,1024]{1,0:T(8,128)(2,1)S(1)} fusion(bf16[1024,512]{0,1:T(8,128)(2,1)S(1)} %maximum_select_fusion, f32[1024,1024]{1,0:T(8,128)S(1)} %get-tuple-element.220, bf16[256,256]{0,1:T(8,128)(2,1)S(1)} %collective-permute-done.44, bf16[256,256]{0,1:T(8,128)(2,1)S(1)} %collective-permute-done.43, ...), kind=kOutput, calls=%fused_computation.15 | convolution fusion | flops 1091567616 | bytes 8388608 | tf_op jit(solution)/shard_map/dot_general | solution.py:28
  262.1 3.9 convolution_convert_fusion.5
  267.4 2.7 convolution_convert_fusion.7
  271.7 2.4 convolution_convert_fusion.8
  274.5 3.5 multiply_reduce_fusion.10
  278.6 2.4 fusion.116
  283.3 19.9 %attention_backward.2 = (bf16[1024,256]{1,0:T(8,128)(2,1)S(1)}, bf16[1024,256]{1,0:T(8,128)(2,1)S(1)}, bf16[1024,256]{1,0:T(8,128)(2,1)S(1)}) custom-call(bf16[1024,768]{1,0:T(8,128)(2,1)S(1)} %copy-done.1, bf16[1024,768]{1,0:T(8,128)(2,1)S(1)} %copy-done.1, bf16[1024,768]{1,0:T(8,128)(2,1)S(1)} %copy-done.1, ...), custom_call_target="tpu_custom_call" | custom-call | tf_op jit(solution)/shard_map/attention_backward/pallas_call | solution.py:210
  313.6 2.6 collective-permute-start.69
  323.7 11.4 %collective-permute-done.69 = bf16[512,256]{0,1:T(8,128)(2,1)} collective-permute-done((bf16[512,256]{0,1:T(8,128)(2,1)}, bf16[512,256]{0,1:T(8,128)(2,1)}, u32[]{:S(2)}, u32[]{:S(2)}) %collective-permute-start.69) | collective-permute-done | bytes 262176 | tf_op jit(solution)/shard_map/ppermute | solution.py:269
  336.4 4.2 all_to_all.163
  342.8 4.3 all_to_all.164
  351.0 3.0 collective-permute-start.63
  354.0 3.6 multiply_reduce_fusion.9
  357.7 3.9 add_convert_fusion.2
  361.7 2.7 fusion.133
  364.4 11.0 %multiply_convert_fusion = bf16[1024,1536]{1,0:T(8,128)(2,1)S(1)} fusion(bf16[1024,768]{1,0:T(8,128)(2,1)S(1)} %get-tuple-element.221, f32[1024,1536]{1,0:T(8,128)S(1)} %bitcast.168, bf16[384,384]{1,0:T(8,128)(2,1)S(1)} %copy-done.119, bf16[384,384]{1,0:T(8,128)(2,1)S(1)} %copy-done.117, bf16[768,384]{1,0:T(8,128)(2,1)} %collective-permute-done.19, ...), kind=kOutput, calls=%fused_computation.6 | convolution fusion | flops 2446589952 | bytes 13369344 | tf_op jit(solution)/shard_map/dot_general | solution.py:28
  375.5 6.4 %convolution_convert_fusion.3 = bf16[1024,768]{0,1:T(8,128)(2,1)} fusion(bf16[1024,1536]{1,0:T(8,128)(2,1)S(1)} %multiply_convert_fusion, bf16[192,768]{1,0:T(8,128)(2,1)S(1)} %copy-done.113, bf16[192,768]{1,0:T(8,128)(2,1)S(1)} %copy-done.115, bf16[384,768]{1,0:T(8,128)(2,1)} %collective-permute-done.15, bf16[384,768]{1,0:T(8,128)(2,1)} %collective-permute-done.14, ...), kind=kOutput, calls=%fused_computation.71 | convolution fusion | flops 2428502016 | bytes 7077888 | tf_op jit(solution)/shard_map/dot_general | solution.py:28
  381.9 3.8 all_to_all.165
  386.2 4.3 all_to_all.166
  391.9 2.5 fusion.42
  394.8 3.6 fusion.45
  401.2 3.6 copy.123
  407.2 5.6 collective-permute-done.60
  417.3 2.8 multiply_reduce_fusion.4
  420.1 3.0 fusion.122
  425.4 16.6 %attention_backward.3 = (bf16[1024,384]{1,0:T(8,128)(2,1)S(1)}, bf16[1024,384]{1,0:T(8,128)(2,1)S(1)}, bf16[1024,384]{1,0:T(8,128)(2,1)S(1)}) custom-call(bf16[1024,1152]{1,0:T(8,128)(2,1)S(1)} %convolution_convert_fusion.q_ref.k_ref.v_ref, bf16[1024,1152]{1,0:T(8,128)(2,1)S(1)} %convolution_convert_fusion.q_ref.k_ref.v_ref, ...), custom_call_target="tpu_custom_call" | custom-call | tf_op jit(solution)/shard_map/attention_backward/pallas_call | solution.py:210
  442.0 2.3 fusion.25
  448.9 2.1 collective-permute-start.52
  451.6 2.2 add_convert_fusion.6
  453.8 23.5 %collective-permute-done.54 = bf16[192,384]{1,0:T(8,128)(2,1)S(1)} collective-permute-done((bf16[192,384]{1,0:T(8,128)(2,1)S(1)}, bf16[192,384]{1,0:T(8,128)(2,1)S(1)}, u32[]{:S(2)}, u32[]{:S(2)}) %collective-permute-start.54) | collective-permute-done | bytes 147488 | tf_op jit(solution)/shard_map/ppermute | solution.py:269
  477.5 3.0 collective-permute-start.53
  481.9 13.6 %collective-permute-done.55 = bf16[192,384]{1,0:T(8,128)(2,1)S(1)} collective-permute-done((bf16[192,384]{1,0:T(8,128)(2,1)S(1)}, bf16[192,384]{1,0:T(8,128)(2,1)S(1)}, u32[]{:S(2)}, u32[]{:S(2)}) %collective-permute-start.55) | collective-permute-done | bytes 147488 | tf_op jit(solution)/shard_map/ppermute | solution.py:269
  496.2 8.7 %collective-permute-done.53 = bf16[384,576]{0,1:T(8,128)(2,1)S(1)} collective-permute-done((bf16[384,576]{0,1:T(8,128)(2,1)S(1)}, bf16[384,576]{0,1:T(8,128)(2,1)S(1)}, u32[]{:S(2)}, u32[]{:S(2)}) %collective-permute-start.53) | collective-permute-done | bytes 442400 | tf_op jit(solution)/shard_map/ppermute | solution.py:269
  508.4 59.6 %all-reduce = (f32[4,384]{1,0:T(4,128)S(1)}, f32[4,512]{1,0:T(4,128)S(1)}) all-reduce(f32[4,384]{1,0:T(4,128)S(1)} %pad_maximum_fusion.6, f32[4,512]{1,0:T(4,128)S(1)} %maximum_select_fusion.1), channel_id=1, replica_groups=mesh['dp'=4,'row'=2,'y'=2,'core'=2] {'dp','y','core'}, use_global_device_ids=true, to_apply=%region_20.21 | all-reduce | flops 3584 | bytes 28672 | tf_op jit(solution)/shard_map/psum | solution.py:553
  (548 shorter events, 151.3 us)
Async XLA Ops:
  7.2 56.3 %all-gather.4.cloned.1.call-start = ((), (), s32[]{:S(2)}) async-start(), calls=%async_computation.8 | async-start | bytes 2359296 | tf_op jit(solution)/shard_map/all_gather | solution.py:360
  7.2 13.5 %collective-permute-start.9 = (bf16[192,384]{1,0:T(8,128)(2,1)}, bf16[192,384]{1,0:T(8,128)(2,1)S(1)}, u32[]{:S(2)}, u32[]{:S(2)}) collective-permute-start(bf16[192,384]{1,0:T(8,128)(2,1)} %param.25), channel_id=1, source_target_pairs={{0,4},{4,0},{1,5},{5,1},{2,6},{6,2},{3,7},{7,3},{8,12},{12,8},{9,1... | collective-permute-start | bytes 442376 | tf_op jit(solution)/shard_map/ppermute | solution.py:36
  10.3 12.2 %collective-permute-start.10 = (bf16[192,384]{1,0:T(8,128)(2,1)}, bf16[192,384]{1,0:T(8,128)(2,1)S(1)}, u32[]{:S(2)}, u32[]{:S(2)}) collective-permute-start(bf16[192,384]{1,0:T(8,128)(2,1)} %param.25), channel_id=1, source_target_pairs={{0,2},{2,0},{1,3},{3,1},{4,6},{6,4},{5,7},{7,5},{8,10},{10,8},{9,1... | collective-permute-start | bytes 442376 | tf_op jit(solution)/shard_map/ppermute | solution.py:36
  11.8 11.3 %collective-permute-start = (bf16[256,384]{1,0:T(8,128)(2,1)}, bf16[256,384]{1,0:T(8,128)(2,1)S(1)}, u32[]{:S(2)}, u32[]{:S(2)}) collective-permute-start(bf16[256,384]{1,0:T(8,128)(2,1)} %param.20), channel_id=1, source_target_pairs={{0,4},{4,0},{1,5},{5,1},{2,6},{6,2},{3,7},{7,3},{8,12},{12,8},{9,1... | collective-permute-start | bytes 589832 | tf_op jit(solution)/shard_map/ppermute | solution.py:36
  12.3 12.3 %collective-permute-start.1 = (bf16[256,384]{1,0:T(8,128)(2,1)}, bf16[256,384]{1,0:T(8,128)(2,1)S(1)}, u32[]{:S(2)}, u32[]{:S(2)}) collective-permute-start(bf16[256,384]{1,0:T(8,128)(2,1)} %param.20), channel_id=1, source_target_pairs={{0,2},{2,0},{1,3},{3,1},{4,6},{6,4},{5,7},{7,5},{8,10},{10,8},{9,1... | collective-permute-start | bytes 589832 | tf_op jit(solution)/shard_map/ppermute | solution.py:36
  19.1 17.3 %collective-permute-start.6 = (bf16[384,576]{0,1:T(8,128)(2,1)}, bf16[384,576]{0,1:T(8,128)(2,1)S(1)}, u32[]{:S(2)}, u32[]{:S(2)}) collective-permute-start(bf16[384,576]{0,1:T(8,128)(2,1)} %bitcast.130), channel_id=1, source_target_pairs={{0,4},{4,0},{1,5},{5,1},{2,6},{6,2},{3,7},{7,3},{8,12},{12,8},{9,1... | collective-permute-start | bytes 1327112 | tf_op jit(solution)/shard_map/ppermute | solution.py:36
  20.8 17.5 %collective-permute-start.5 = (bf16[384,576]{0,1:T(8,128)(2,1)}, bf16[384,576]{0,1:T(8,128)(2,1)S(1)}, u32[]{:S(2)}, u32[]{:S(2)}) collective-permute-start(bf16[384,576]{0,1:T(8,128)(2,1)} %bitcast.131), channel_id=1, source_target_pairs={{0,2},{2,0},{1,3},{3,1},{4,6},{6,4},{5,7},{7,5},{8,10},{10,8},{9,1... | collective-permute-start | bytes 1327112 | tf_op jit(solution)/shard_map/ppermute | solution.py:36
  22.5 75.7 %collective-permute-start.11 = (bf16[96,384]{1,0:T(8,128)(2,1)S(1)}, bf16[96,384]{1,0:T(8,128)(2,1)}, u32[]{:S(2)}, u32[]{:S(2)}) collective-permute-start(bf16[96,384]{1,0:T(8,128)(2,1)S(1)} %slice.377), channel_id=1, source_target_pairs={{0,2},{2,0},{1,3},{3,1},{4,6},{6,4},{5,7},{7,5},{8,10},{10,8},{9,1... | collective-permute-start | bytes 221192 | tf_op jit(solution)/shard_map/ppermute | solution.py:36
  23.1 12.1 %collective-permute-start.2 = (bf16[128,384]{1,0:T(8,128)(2,1)S(1)}, bf16[128,384]{1,0:T(8,128)(2,1)S(1)}, u32[]{:S(2)}, u32[]{:S(2)}) collective-permute-start(bf16[128,384]{1,0:T(8,128)(2,1)S(1)} %slice.358), channel_id=1, source_target_pairs={{0,2},{2,0},{1,3},{3,1},{4,6},{6,4},{5,7},{7,5},{8,10},{10,8},{9,1... | collective-permute-start | bytes 294920 | tf_op jit(solution)/shard_map/ppermute | solution.py:36
  24.7 10.8 %collective-permute-start.3 = (bf16[128,384]{1,0:T(8,128)(2,1)S(1)}, bf16[128,384]{1,0:T(8,128)(2,1)S(1)}, u32[]{:S(2)}, u32[]{:S(2)}) collective-permute-start(bf16[128,384]{1,0:T(8,128)(2,1)S(1)} %slice.359), channel_id=1, source_target_pairs={{0,4},{4,0},{1,5},{5,1},{2,6},{6,2},{3,7},{7,3},{8,12},{12,8},{9,1... | collective-permute-start | bytes 294920 | tf_op jit(solution)/shard_map/ppermute | solution.py:36
  35.1 63.0 %collective-permute-start.12 = (bf16[96,384]{1,0:T(8,128)(2,1)S(1)}, bf16[96,384]{1,0:T(8,128)(2,1)}, u32[]{:S(2)}, u32[]{:S(2)}) collective-permute-start(bf16[96,384]{1,0:T(8,128)(2,1)S(1)} %slice.378), channel_id=1, source_target_pairs={{0,4},{4,0},{1,5},{5,1},{2,6},{6,2},{3,7},{7,3},{8,12},{12,8},{9,1... | collective-permute-start | bytes 221192 | tf_op jit(solution)/shard_map/ppermute | solution.py:36
  101.9 39.5 %collective-permute-start.13 = (bf16[1024,768]{0,1:T(8,128)(2,1)}, bf16[1024,768]{0,1:T(8,128)(2,1)}, u32[]{:S(2)}, u32[]{:S(2)}) collective-permute-start(bf16[1024,768]{0,1:T(8,128)(2,1)} %convolution_convert_fusion.2), channel_id=1, source_target_pairs={{0,1},{1,0},{2,3},{3,2},{4,5},{5,4},{6,7},{7,6},{8,9},{9,8},{10,11... | collective-permute-start | bytes 4718600 | tf_op jit(solution)/shard_map/ppermute | solution.py:36
  102.0 8.5 %collective-permute-start.23 = (bf16[384,128]{1,0:T(8,128)(2,1)S(1)}, bf16[384,128]{1,0:T(8,128)(2,1)S(1)}, u32[]{:S(2)}, u32[]{:S(2)}) collective-permute-start(bf16[384,128]{1,0:T(8,128)(2,1)S(1)} %copy-done.56), channel_id=1, source_target_pairs={{0,2},{2,0},{1,3},{3,1},{4,6},{6,4},{5,7},{7,5},{8,10},{10,8},{9,1... | collective-permute-start | bytes 294920 | tf_op jit(solution)/shard_map/ppermute | solution.py:36
  102.3 9.2 %collective-permute-start.24 = (bf16[384,128]{1,0:T(8,128)(2,1)S(1)}, bf16[384,128]{1,0:T(8,128)(2,1)S(1)}, u32[]{:S(2)}, u32[]{:S(2)}) collective-permute-start(bf16[384,128]{1,0:T(8,128)(2,1)S(1)} %copy-done.56), channel_id=1, source_target_pairs={{0,4},{4,0},{1,5},{5,1},{2,6},{6,2},{3,7},{7,3},{8,12},{12,8},{9,1... | collective-permute-start | bytes 294920 | tf_op jit(solution)/shard_map/ppermute | solution.py:36
  107.4 17.2 %collective-permute-start.14 = (bf16[384,768]{1,0:T(8,128)(2,1)}, bf16[384,768]{1,0:T(8,128)(2,1)}, u32[]{:S(2)}, u32[]{:S(2)}) collective-permute-start(bf16[384,768]{1,0:T(8,128)(2,1)} %param.28), channel_id=1, source_target_pairs={{0,2},{2,0},{1,3},{3,1},{4,6},{6,4},{5,7},{7,5},{8,10},{10,8},{9,1... | collective-permute-start | bytes 1769480 | tf_op jit(solution)/shard_map/ppermute | solution.py:36
  109.5 16.6 %collective-permute-start.15 = (bf16[384,768]{1,0:T(8,128)(2,1)}, bf16[384,768]{1,0:T(8,128)(2,1)}, u32[]{:S(2)}, u32[]{:S(2)}) collective-permute-start(bf16[384,768]{1,0:T(8,128)(2,1)} %param.28), channel_id=1, source_target_pairs={{0,4},{4,0},{1,5},{5,1},{2,6},{6,2},{3,7},{7,3},{8,12},{12,8},{9,1... | collective-permute-start | bytes 1769480 | tf_op jit(solution)/shard_map/ppermute | solution.py:36
  110.5 26.9 %collective-permute-start.18 = (bf16[768,384]{1,0:T(8,128)(2,1)}, bf16[768,384]{1,0:T(8,128)(2,1)}, u32[]{:S(2)}, u32[]{:S(2)}) collective-permute-start(bf16[768,384]{1,0:T(8,128)(2,1)} %param.29), channel_id=1, source_target_pairs={{0,4},{4,0},{1,5},{5,1},{2,6},{6,2},{3,7},{7,3},{8,12},{12,8},{9,1... | collective-permute-start | bytes 1769480 | tf_op jit(solution)/shard_map/ppermute | solution.py:36
  111.5 27.8 %collective-permute-start.19 = (bf16[768,384]{1,0:T(8,128)(2,1)}, bf16[768,384]{1,0:T(8,128)(2,1)}, u32[]{:S(2)}, u32[]{:S(2)}) collective-permute-start(bf16[768,384]{1,0:T(8,128)(2,1)} %param.29), channel_id=1, source_target_pairs={{0,2},{2,0},{1,3},{3,1},{4,6},{6,4},{5,7},{7,5},{8,10},{10,8},{9,1... | collective-permute-start | bytes 1769480 | tf_op jit(solution)/shard_map/ppermute | solution.py:36
  124.6 42.4 %collective-permute-start.33 = (bf16[128,256]{0,1:T(8,128)(2,1)S(1)}, bf16[128,256]{0,1:T(8,128)(2,1)S(1)}, u32[]{:S(2)}, u32[]{:S(2)}) collective-permute-start(bf16[128,256]{0,1:T(8,128)(2,1)S(1)} %bitcast.138), channel_id=1, source_target_pairs={{0,4},{4,0},{1,5},{5,1},{2,6},{6,2},{3,7},{7,3},{8,12},{12,8},{9,1... | collective-permute-start | bytes 196616 | tf_op jit(solution)/shard_map/ppermute | solution.py:36
  126.1 39.7 %collective-permute-start.32 = (bf16[128,256]{0,1:T(8,128)(2,1)S(1)}, bf16[128,256]{0,1:T(8,128)(2,1)S(1)}, u32[]{:S(2)}, u32[]{:S(2)}) collective-permute-start(bf16[128,256]{0,1:T(8,128)(2,1)S(1)} %bitcast.139), channel_id=1, source_target_pairs={{0,2},{2,0},{1,3},{3,1},{4,6},{6,4},{5,7},{7,5},{8,10},{10,8},{9,1... | collective-permute-start | bytes 196616 | tf_op jit(solution)/shard_map/ppermute | solution.py:36
  137.4 31.8 %collective-permute-start.26 = (bf16[192,128]{1,0:T(8,128)(2,1)S(1)}, bf16[192,128]{1,0:T(8,128)(2,1)S(1)}, u32[]{:S(2)}, u32[]{:S(2)}) collective-permute-start(bf16[192,128]{1,0:T(8,128)(2,1)S(1)} %slice.386), channel_id=1, source_target_pairs={{0,4},{4,0},{1,5},{5,1},{2,6},{6,2},{3,7},{7,3},{8,12},{12,8},{9,1... | collective-permute-start | bytes 147464 | tf_op jit(solution)/shard_map/ppermute | solution.py:36
  139.3 8.8 %collective-permute-start.17 = (bf16[192,768]{1,0:T(8,128)(2,1)S(1)}, bf16[192,768]{1,0:T(8,128)(2,1)S(1)}, u32[]{:S(2)}, u32[]{:S(2)}) collective-permute-start(bf16[192,768]{1,0:T(8,128)(2,1)S(1)} %slice.382), channel_id=1, source_target_pairs={{0,4},{4,0},{1,5},{5,1},{2,6},{6,2},{3,7},{7,3},{8,12},{12,8},{9,1... | collective-permute-start | bytes 884744 | tf_op jit(solution)/shard_map/ppermute | solution.py:36
  141.5 7.8 %collective-permute-start.16 = (bf16[192,768]{1,0:T(8,128)(2,1)S(1)}, bf16[192,768]{1,0:T(8,128)(2,1)S(1)}, u32[]{:S(2)}, u32[]{:S(2)}) collective-permute-start(bf16[192,768]{1,0:T(8,128)(2,1)S(1)} %slice.381), channel_id=1, source_target_pairs={{0,2},{2,0},{1,3},{3,1},{4,6},{6,4},{5,7},{7,5},{8,10},{10,8},{9,1... | collective-permute-start | bytes 884744 | tf_op jit(solution)/shard_map/ppermute | solution.py:36
  148.1 11.5 %collective-permute-start.20 = (bf16[384,384]{1,0:T(8,128)(2,1)S(1)}, bf16[384,384]{1,0:T(8,128)(2,1)S(1)}, u32[]{:S(2)}, u32[]{:S(2)}) collective-permute-start(bf16[384,384]{1,0:T(8,128)(2,1)S(1)} %slice.383), channel_id=1, source_target_pairs={{0,2},{2,0},{1,3},{3,1},{4,6},{6,4},{5,7},{7,5},{8,10},{10,8},{9,1... | collective-permute-start | bytes 884744 | tf_op jit(solution)/shard_map/ppermute | solution.py:36
  149.3 11.7 %collective-permute-start.21 = (bf16[384,384]{1,0:T(8,128)(2,1)S(1)}, bf16[384,384]{1,0:T(8,128)(2,1)S(1)}, u32[]{:S(2)}, u32[]{:S(2)}) collective-permute-start(bf16[384,384]{1,0:T(8,128)(2,1)S(1)} %slice.384), channel_id=1, source_target_pairs={{0,4},{4,0},{1,5},{5,1},{2,6},{6,2},{3,7},{7,3},{8,12},{12,8},{9,1... | collective-permute-start | bytes 884744 | tf_op jit(solution)/shard_map/ppermute | solution.py:36
  159.6 10.4 %collective-permute-start.25 = (bf16[192,128]{1,0:T(8,128)(2,1)S(1)}, bf16[192,128]{1,0:T(8,128)(2,1)S(1)}, u32[]{:S(2)}, u32[]{:S(2)}) collective-permute-start(bf16[192,128]{1,0:T(8,128)(2,1)S(1)} %slice.385), channel_id=1, source_target_pairs={{0,2},{2,0},{1,3},{3,1},{4,6},{6,4},{5,7},{7,5},{8,10},{10,8},{9,1... | collective-permute-start | bytes 147464 | tf_op jit(solution)/shard_map/ppermute | solution.py:36
  165.2 15.2 %collective-permute-start.22 = (bf16[1024,768]{0,1:T(8,128)(2,1)S(1)}, bf16[1024,768]{0,1:T(8,128)(2,1)S(1)}, u32[]{:S(2)}, u32[]{:S(2)}) collective-permute-start(bf16[1024,768]{0,1:T(8,128)(2,1)S(1)} %convolution_convert_fusion.4), channel_id=1, source_target_pairs={{0,1},{1,0},{2,3},{3,2},{4,5},{5,4},{6,7},{7,6},{8,9},{9,8},{10,11... | collective-permute-start | bytes 4718600 | tf_op jit(solution)/shard_map/ppermute | solution.py:36
  167.1 8.5 %collective-permute-start.28 = (bf16[256,384]{0,1:T(8,128)(2,1)S(1)}, bf16[256,384]{0,1:T(8,128)(2,1)S(1)}, u32[]{:S(2)}, u32[]{:S(2)}) collective-permute-start(bf16[256,384]{0,1:T(8,128)(2,1)S(1)} %bitcast.125), channel_id=1, source_target_pairs={{0,4},{4,0},{1,5},{5,1},{2,6},{6,2},{3,7},{7,3},{8,12},{12,8},{9,1... | collective-permute-start | bytes 589832 | tf_op jit(solution)/shard_map/ppermute | solution.py:36
  169.1 30.8 %collective-permute-start.34 = (bf16[64,256]{0,1:T(8,128)(2,1)S(1)}, bf16[64,256]{0,1:T(8,128)(2,1)S(1)}, u32[]{:S(2)}, u32[]{:S(2)}) collective-permute-start(bf16[64,256]{0,1:T(8,128)(2,1)S(1)} %bitcast.166), channel_id=1, source_target_pairs={{0,2},{2,0},{1,3},{3,1},{4,6},{6,4},{5,7},{7,5},{8,10},{10,8},{9,1... | collective-permute-start | bytes 98312 | tf_op jit(solution)/shard_map/ppermute | solution.py:36
  170.0 29.9 %collective-permute-start.35 = (bf16[64,256]{0,1:T(8,128)(2,1)S(1)}, bf16[64,256]{0,1:T(8,128)(2,1)S(1)}, u32[]{:S(2)}, u32[]{:S(2)}) collective-permute-start(bf16[64,256]{0,1:T(8,128)(2,1)S(1)} %slice.408), channel_id=1, source_target_pairs={{0,4},{4,0},{1,5},{5,1},{2,6},{6,2},{3,7},{7,3},{8,12},{12,8},{9,1... | collective-permute-start | bytes 98312 | tf_op jit(solution)/shard_map/ppermute | solution.py:36
  201.4 45.4 %collective-permute-start.36 = (bf16[1024,512]{0,1:T(8,128)(2,1)}, bf16[1024,512]{0,1:T(8,128)(2,1)}, u32[]{:S(2)}, u32[]{:S(2)}) collective-permute-start(bf16[1024,512]{0,1:T(8,128)(2,1)} %convolution_convert_fusion.6), channel_id=1, source_target_pairs={{0,1},{1,0},{2,3},{3,2},{4,5},{5,4},{6,7},{7,6},{8,9},{9,8},{10,11... | collective-permute-start | bytes 3145736 | tf_op jit(solution)/shard_map/ppermute | solution.py:36
  204.4 8.7 %collective-permute-start.46 = (bf16[512,256]{0,1:T(8,128)(2,1)}, bf16[512,256]{0,1:T(8,128)(2,1)}, u32[]{:S(2)}, u32[]{:S(2)}) collective-permute-start(bf16[512,256]{0,1:T(8,128)(2,1)} %all_gather.23), channel_id=1, source_target_pairs={{0,2},{2,0},{1,3},{3,1},{4,6},{6,4},{5,7},{7,5},{8,10},{10,8},{9,1... | collective-permute-start | bytes 786440 | tf_op jit(solution)/shard_map/ppermute | solution.py:36
  210.6 14.4 %collective-permute-start.38 = (bf16[256,512]{1,0:T(8,128)(2,1)}, bf16[256,512]{1,0:T(8,128)(2,1)}, u32[]{:S(2)}, u32[]{:S(2)}) collective-permute-start(bf16[256,512]{1,0:T(8,128)(2,1)} %bitcast.25), channel_id=1, source_target_pairs={{0,2},{2,0},{1,3},{3,1},{4,6},{6,4},{5,7},{7,5},{8,10},{10,8},{9,1... | collective-permute-start | bytes 786440 | tf_op jit(solution)/shard_map/ppermute | solution.py:36
  214.0 29.8 %collective-permute-start.47 = (bf16[512,512]{0,1:T(8,128)(2,1)S(1)}, bf16[512,512]{0,1:T(8,128)(2,1)}, u32[]{:S(2)}, u32[]{:S(2)}) collective-permute-start(bf16[512,512]{0,1:T(8,128)(2,1)S(1)} %constant_dynamic-update-slice_fusion.4), channel_id=1, source_target_pairs={{0,4},{4,0},{1,5},{5,1},{2,6},{6,2},{3,7},{7,3},{8,12},{12,8},{9,1... | collective-permute-start | bytes 1572872 | tf_op jit(solution)/shard_map/ppermute | solution.py:36
  215.4 19.3 %collective-permute-start.37 = (bf16[256,512]{1,0:T(8,128)(2,1)}, bf16[256,512]{1,0:T(8,128)(2,1)}, u32[]{:S(2)}, u32[]{:S(2)}) collective-permute-start(bf16[256,512]{1,0:T(8,128)(2,1)} %bitcast.25), channel_id=1, source_target_pairs={{0,4},{4,0},{1,5},{5,1},{2,6},{6,2},{3,7},{7,3},{8,12},{12,8},{9,1... | collective-permute-start | bytes 786440 | tf_op jit(solution)/shard_map/ppermute | solution.py:36
  223.7 16.2 %collective-permute-start.42 = (bf16[512,256]{0,1:T(8,128)(2,1)}, bf16[512,256]{0,1:T(8,128)(2,1)}, u32[]{:S(2)}, u32[]{:S(2)}) collective-permute-start(bf16[512,256]{0,1:T(8,128)(2,1)} %bitcast.133), channel_id=1, source_target_pairs={{0,4},{4,0},{1,5},{5,1},{2,6},{6,2},{3,7},{7,3},{8,12},{12,8},{9,1... | collective-permute-start | bytes 786440 | tf_op jit(solution)/shard_map/ppermute | solution.py:36
  225.0 17.0 %collective-permute-start.41 = (bf16[512,256]{0,1:T(8,128)(2,1)}, bf16[512,256]{0,1:T(8,128)(2,1)}, u32[]{:S(2)}, u32[]{:S(2)}) collective-permute-start(bf16[512,256]{0,1:T(8,128)(2,1)} %bitcast.134), channel_id=1, source_target_pairs={{0,2},{2,0},{1,3},{3,1},{4,6},{6,4},{5,7},{7,5},{8,10},{10,8},{9,1... | collective-permute-start | bytes 786440 | tf_op jit(solution)/shard_map/ppermute | solution.py:36
  234.7 16.7 %collective-permute-start.40 = (bf16[128,512]{1,0:T(8,128)(2,1)S(1)}, bf16[128,512]{1,0:T(8,128)(2,1)S(1)}, u32[]{:S(2)}, u32[]{:S(2)}) collective-permute-start(bf16[128,512]{1,0:T(8,128)(2,1)S(1)} %slice.412), channel_id=1, source_target_pairs={{0,4},{4,0},{1,5},{5,1},{2,6},{6,2},{3,7},{7,3},{8,12},{12,8},{9,1... | collective-permute-start | bytes 393224 | tf_op jit(solution)/shard_map/ppermute | solution.py:36
  239.9 11.5 %collective-permute-start.39 = (bf16[128,512]{1,0:T(8,128)(2,1)S(1)}, bf16[128,512]{1,0:T(8,128)(2,1)S(1)}, u32[]{:S(2)}, u32[]{:S(2)}) collective-permute-start(bf16[128,512]{1,0:T(8,128)(2,1)S(1)} %slice.411), channel_id=1, source_target_pairs={{0,2},{2,0},{1,3},{3,1},{4,6},{6,4},{5,7},{7,5},{8,10},{10,8},{9,1... | collective-permute-start | bytes 393224 | tf_op jit(solution)/shard_map/ppermute | solution.py:36
  242.0 13.9 %collective-permute-start.43 = (bf16[256,256]{0,1:T(8,128)(2,1)S(1)}, bf16[256,256]{0,1:T(8,128)(2,1)S(1)}, u32[]{:S(2)}, u32[]{:S(2)}) collective-permute-start(bf16[256,256]{0,1:T(8,128)(2,1)S(1)} %slice.413), channel_id=1, source_target_pairs={{0,2},{2,0},{1,3},{3,1},{4,6},{6,4},{5,7},{7,5},{8,10},{10,8},{9,1... | collective-permute-start | bytes 393224 | tf_op jit(solution)/shard_map/ppermute | solution.py:36
  243.9 12.1 %collective-permute-start.44 = (bf16[256,256]{0,1:T(8,128)(2,1)S(1)}, bf16[256,256]{0,1:T(8,128)(2,1)S(1)}, u32[]{:S(2)}, u32[]{:S(2)}) collective-permute-start(bf16[256,256]{0,1:T(8,128)(2,1)S(1)} %slice.414), channel_id=1, source_target_pairs={{0,4},{4,0},{1,5},{5,1},{2,6},{6,2},{3,7},{7,3},{8,12},{12,8},{9,1... | collective-permute-start | bytes 393224 | tf_op jit(solution)/shard_map/ppermute | solution.py:36
  266.0 8.5 %collective-permute-start.48 = (bf16[1024,512]{0,1:T(8,128)(2,1)}, bf16[1024,512]{0,1:T(8,128)(2,1)}, u32[]{:S(2)}, u32[]{:S(2)}) collective-permute-start(bf16[1024,512]{0,1:T(8,128)(2,1)} %convolution_convert_fusion.5), channel_id=1, source_target_pairs={{0,1},{1,0},{2,3},{3,2},{4,5},{5,4},{6,7},{7,6},{8,9},{9,8},{10,11... | collective-permute-start | bytes 3145736 | tf_op jit(solution)/shard_map/ppermute | solution.py:36
  270.1 41.5 %collective-permute-start.68 = (bf16[512,256]{0,1:T(8,128)(2,1)}, bf16[512,256]{0,1:T(8,128)(2,1)}, u32[]{:S(2)}, u32[]{:S(2)}) collective-permute-start(bf16[512,256]{0,1:T(8,128)(2,1)} %convolution_convert_fusion.7), channel_id=1, source_target_pairs={{0,8},{8,0},{16,24},{24,16},{1,9},{9,1},{17,25},{25,17},{2,10},{10... | collective-permute-start | bytes 786440 | tf_op jit(solution)/shard_map/ppermute | solution.py:269
  274.1 42.1 %collective-permute-start.66 = (bf16[256,512]{1,0:T(8,128)(2,1)}, bf16[256,512]{1,0:T(8,128)(2,1)}, u32[]{:S(2)}, u32[]{:S(2)}) collective-permute-start(bf16[256,512]{1,0:T(8,128)(2,1)} %convolution_convert_fusion.8), channel_id=1, source_target_pairs={{0,8},{8,0},{16,24},{24,16},{1,9},{9,1},{17,25},{25,17},{2,10},{10... | collective-permute-start | bytes 786440 | tf_op jit(solution)/shard_map/ppermute | solution.py:269
  305.4 48.6 %collective-permute-start.49 = (bf16[1024,512]{0,1:T(8,128)(2,1)}, bf16[1024,512]{0,1:T(8,128)(2,1)}, u32[]{:S(2)}, u32[]{:S(2)}) collective-permute-start(bf16[1024,512]{0,1:T(8,128)(2,1)} %fusion.39), channel_id=1, source_target_pairs={{0,1},{1,0},{2,3},{3,2},{4,5},{5,4},{6,7},{7,6},{8,9},{9,8},{10,11... | collective-permute-start | bytes 3145736 | tf_op jit(solution)/shard_map/ppermute | solution.py:36
  311.0 10.4 %collective-permute-start.45 = (bf16[512,128]{0,1:T(8,128)(2,1)S(1)}, bf16[512,128]{0,1:T(8,128)(2,1)S(1)}, u32[]{:S(2)}, u32[]{:S(2)}) collective-permute-start(bf16[512,128]{0,1:T(8,128)(2,1)S(1)} %dynamic-slice_convert_fusion), channel_id=1, source_target_pairs={{0,1},{1,0},{2,3},{3,2},{4,5},{5,4},{6,7},{7,6},{8,9},{9,8},{10,11... | collective-permute-start | bytes 393224 | tf_op jit(solution)/shard_map/ppermute | solution.py:36
  313.6 21.6 %collective-permute-start.69 = (bf16[512,256]{0,1:T(8,128)(2,1)}, bf16[512,256]{0,1:T(8,128)(2,1)}, u32[]{:S(2)}, u32[]{:S(2)}) collective-permute-start(bf16[512,256]{0,1:T(8,128)(2,1)} %add.290), channel_id=1, source_target_pairs={{0,16},{8,24},{16,0},{24,8},{1,17},{9,25},{17,1},{25,9},{2,18},{10... | collective-permute-start | bytes 786440 | tf_op jit(solution)/shard_map/ppermute | solution.py:269
  318.0 23.5 %collective-permute-start.67 = (bf16[256,512]{1,0:T(8,128)(2,1)}, bf16[256,512]{1,0:T(8,128)(2,1)}, u32[]{:S(2)}, u32[]{:S(2)}) collective-permute-start(bf16[256,512]{1,0:T(8,128)(2,1)} %add.288), channel_id=1, source_target_pairs={{0,16},{8,24},{16,0},{24,8},{1,17},{9,25},{17,1},{25,9},{2,18},{10... | collective-permute-start | bytes 786440 | tf_op jit(solution)/shard_map/ppermute | solution.py:269
  318.7 31.1 %collective-permute-start.64 = (bf16[128,256]{1,0:T(8,128)(2,1)S(1)}, bf16[128,256]{1,0:T(8,128)(2,1)S(1)}, u32[]{:S(2)}, u32[]{:S(2)}) collective-permute-start(bf16[128,256]{1,0:T(8,128)(2,1)S(1)} %convolution_convert_fusion.12), channel_id=1, source_target_pairs={{0,8},{8,0},{16,24},{24,16},{1,9},{9,1},{17,25},{25,17},{2,10},{10... | collective-permute-start | bytes 196616 | tf_op jit(solution)/shard_map/ppermute | solution.py:269
  321.5 28.5 %collective-permute-start.62 = (bf16[256,384]{1,0:T(8,128)(2,1)}, bf16[256,384]{1,0:T(8,128)(2,1)}, u32[]{:S(2)}, u32[]{:S(2)}) collective-permute-start(bf16[256,384]{1,0:T(8,128)(2,1)} %convolution_convert_fusion.9), channel_id=1, source_target_pairs={{0,8},{8,0},{16,24},{24,16},{1,9},{9,1},{17,25},{25,17},{2,10},{10... | collective-permute-start | bytes 589832 | tf_op jit(solution)/shard_map/ppermute | solution.py:269
  349.8 32.0 %collective-permute-start.65 = (bf16[128,256]{1,0:T(8,128)(2,1)S(1)}, bf16[128,256]{1,0:T(8,128)(2,1)S(1)}, u32[]{:S(2)}, u32[]{:S(2)}) collective-permute-start(bf16[128,256]{1,0:T(8,128)(2,1)S(1)} %add.286), channel_id=1, source_target_pairs={{0,16},{8,24},{16,0},{24,8},{1,17},{9,25},{17,1},{25,9},{2,18},{10... | collective-permute-start | bytes 196616 | tf_op jit(solution)/shard_map/ppermute | solution.py:269
  351.0 34.7 %collective-permute-start.63 = (bf16[256,384]{1,0:T(8,128)(2,1)S(1)}, bf16[256,384]{1,0:T(8,128)(2,1)S(1)}, u32[]{:S(2)}, u32[]{:S(2)}) collective-permute-start(bf16[256,384]{1,0:T(8,128)(2,1)S(1)} %add.284), channel_id=1, source_target_pairs={{0,16},{8,24},{16,0},{24,8},{1,17},{9,25},{17,1},{25,9},{2,18},{10... | collective-permute-start | bytes 589832 | tf_op jit(solution)/shard_map/ppermute | solution.py:269
  381.8 35.4 %collective-permute-start.50 = (bf16[1024,768]{0,1:T(8,128)(2,1)}, bf16[1024,768]{0,1:T(8,128)(2,1)}, u32[]{:S(2)}, u32[]{:S(2)}) collective-permute-start(bf16[1024,768]{0,1:T(8,128)(2,1)} %convolution_convert_fusion.3), channel_id=1, source_target_pairs={{0,1},{1,0},{2,3},{3,2},{4,5},{5,4},{6,7},{7,6},{8,9},{9,8},{10,11... | collective-permute-start | bytes 4718600 | tf_op jit(solution)/shard_map/ppermute | solution.py:36
  394.4 19.6 %collective-permute-start.56 = (bf16[384,768]{1,0:T(8,128)(2,1)S(1)}, bf16[384,768]{1,0:T(8,128)(2,1)}, u32[]{:S(2)}, u32[]{:S(2)}) collective-permute-start(bf16[384,768]{1,0:T(8,128)(2,1)S(1)} %fusion.42), channel_id=1, source_target_pairs={{0,8},{8,0},{16,24},{24,16},{1,9},{9,1},{17,25},{25,17},{2,10},{10... | collective-permute-start | bytes 1769480 | tf_op jit(solution)/shard_map/ppermute | solution.py:269
  399.7 13.1 %collective-permute-start.60 = (bf16[384,128]{1,0:T(8,128)(2,1)S(1)}, bf16[384,128]{1,0:T(8,128)(2,1)S(1)}, u32[]{:S(2)}, u32[]{:S(2)}) collective-permute-start(bf16[384,128]{1,0:T(8,128)(2,1)S(1)} %convolution_convert_fusion.11), channel_id=1, source_target_pairs={{0,8},{8,0},{16,24},{24,16},{1,9},{9,1},{17,25},{25,17},{2,10},{10... | collective-permute-start | bytes 294920 | tf_op jit(solution)/shard_map/ppermute | solution.py:269
  404.8 40.3 %collective-permute-start.58 = (bf16[768,384]{1,0:T(8,128)(2,1)}, bf16[768,384]{1,0:T(8,128)(2,1)S(1)}, u32[]{:S(2)}, u32[]{:S(2)}) collective-permute-start(bf16[768,384]{1,0:T(8,128)(2,1)} %fusion.45), channel_id=1, source_target_pairs={{0,8},{8,0},{16,24},{24,16},{1,9},{9,1},{17,25},{25,17},{2,10},{10... | collective-permute-start | bytes 1769480 | tf_op jit(solution)/shard_map/ppermute | solution.py:269
  412.8 31.5 %collective-permute-start.61 = (bf16[384,128]{1,0:T(8,128)(2,1)S(1)}, bf16[384,128]{1,0:T(8,128)(2,1)S(1)}, u32[]{:S(2)}, u32[]{:S(2)}) collective-permute-start(bf16[384,128]{1,0:T(8,128)(2,1)S(1)} %add.281), channel_id=1, source_target_pairs={{0,16},{8,24},{16,0},{24,8},{1,17},{9,25},{17,1},{25,9},{2,18},{10... | collective-permute-start | bytes 294920 | tf_op jit(solution)/shard_map/ppermute | solution.py:269
  415.4 36.2 %collective-permute-start.57 = (bf16[384,768]{1,0:T(8,128)(2,1)S(1)}, bf16[384,768]{1,0:T(8,128)(2,1)}, u32[]{:S(2)}, u32[]{:S(2)}) collective-permute-start(bf16[384,768]{1,0:T(8,128)(2,1)S(1)} %add.277), channel_id=1, source_target_pairs={{0,16},{8,24},{16,0},{24,8},{1,17},{9,25},{17,1},{25,9},{2,18},{10... | collective-permute-start | bytes 1769480 | tf_op jit(solution)/shard_map/ppermute | solution.py:269
  444.3 61.7 %collective-permute-start.51 = (bf16[1024,768]{0,1:T(8,128)(2,1)S(1)}, bf16[1024,768]{0,1:T(8,128)(2,1)S(1)}, u32[]{:S(2)}, u32[]{:S(2)}) collective-permute-start(bf16[1024,768]{0,1:T(8,128)(2,1)S(1)} %fusion.25), channel_id=1, source_target_pairs={{0,1},{1,0},{2,3},{3,2},{4,5},{5,4},{6,7},{7,6},{8,9},{9,8},{10,11... | collective-permute-start | bytes 4718600 | tf_op jit(solution)/shard_map/ppermute | solution.py:36
  446.4 34.1 %collective-permute-start.59 = (bf16[768,384]{1,0:T(8,128)(2,1)S(1)}, bf16[768,384]{1,0:T(8,128)(2,1)S(1)}, u32[]{:S(2)}, u32[]{:S(2)}) collective-permute-start(bf16[768,384]{1,0:T(8,128)(2,1)S(1)} %add.279), channel_id=1, source_target_pairs={{0,16},{8,24},{16,0},{24,8},{1,17},{9,25},{17,1},{25,9},{2,18},{10... | collective-permute-start | bytes 1769480 | tf_op jit(solution)/shard_map/ppermute | solution.py:269
  448.9 28.5 %collective-permute-start.52 = (bf16[384,576]{0,1:T(8,128)(2,1)S(1)}, bf16[384,576]{0,1:T(8,128)(2,1)S(1)}, u32[]{:S(2)}, u32[]{:S(2)}) collective-permute-start(bf16[384,576]{0,1:T(8,128)(2,1)S(1)} %fusion.54), channel_id=1, source_target_pairs={{0,8},{8,0},{16,24},{24,16},{1,9},{9,1},{17,25},{25,17},{2,10},{10... | collective-permute-start | bytes 1327112 | tf_op jit(solution)/shard_map/ppermute | solution.py:269
  451.5 25.7 %collective-permute-start.54 = (bf16[192,384]{1,0:T(8,128)(2,1)S(1)}, bf16[192,384]{1,0:T(8,128)(2,1)S(1)}, u32[]{:S(2)}, u32[]{:S(2)}) collective-permute-start(bf16[192,384]{1,0:T(8,128)(2,1)S(1)} %convolution_convert_fusion.10), channel_id=1, source_target_pairs={{0,8},{8,0},{16,24},{24,16},{1,9},{9,1},{17,25},{25,17},{2,10},{10... | collective-permute-start | bytes 442376 | tf_op jit(solution)/shard_map/ppermute | solution.py:269
  477.3 18.1 %collective-permute-start.55 = (bf16[192,384]{1,0:T(8,128)(2,1)S(1)}, bf16[192,384]{1,0:T(8,128)(2,1)S(1)}, u32[]{:S(2)}, u32[]{:S(2)}) collective-permute-start(bf16[192,384]{1,0:T(8,128)(2,1)S(1)} %add.275), channel_id=1, source_target_pairs={{0,16},{8,24},{16,0},{24,8},{1,17},{9,25},{17,1},{25,9},{2,18},{10... | collective-permute-start | bytes 442376 | tf_op jit(solution)/shard_map/ppermute | solution.py:269
  477.5 27.3 %collective-permute-start.53 = (bf16[384,576]{0,1:T(8,128)(2,1)S(1)}, bf16[384,576]{0,1:T(8,128)(2,1)S(1)}, u32[]{:S(2)}, u32[]{:S(2)}) collective-permute-start(bf16[384,576]{0,1:T(8,128)(2,1)S(1)} %add.273), channel_id=1, source_target_pairs={{0,16},{8,24},{16,0},{24,8},{1,17},{9,25},{17,1},{25,9},{2,18},{10... | collective-permute-start | bytes 1327112 | tf_op jit(solution)/shard_map/ppermute | solution.py:269
  (145 other events, 1517.9 us)
Sparse Core Ops, SparseCore 0:
  36.6 11.2 all-gather.3
